TPU v7x, 32 devices: a whole 2x2x4 slice. The times are simulated.
32 devices in a mesh: lon: 8 (over z, core), lat: 4 (over y, x).
Axes of the slice: x: 2, y: 2, z: 4, core: 2. Of those that a mesh axis runs over, the one named last changes fastest.
Arguments:
- state: bfloat16 [96, 384, 512], P('lat', 'lon'), may hold values from -6 to 6
- attention_in: bfloat16 [2, 512, 1536], replicated, may hold values from -10 to 10
- attention_out: bfloat16 [2, 512, 512], replicated, may hold values from -0.25 to 0.25
- expand_weight: bfloat16 [2, 512, 2048], replicated, may hold values from -0.25 to 0.25
- depth_kernel: bfloat16 [2, 7, 7, 2048], replicated, may hold values from -0.875 to 0.875
- shrink_weight: bfloat16 [2, 2048, 512], replicated, may hold values from -0.125 to 0.125
- norm_attention: float32 [2, 512], replicated, may hold values from 0.1 to 1.9
- norm_feedforward: float32 [2, 512], replicated, may hold values from 0.1 to 1.9
Outputs:
- advanced_state: bfloat16 [96, 384, 512], P('lat', 'lon')
All inputs are finite; a program needn't handle non-finite values.
Results may differ from a plain program's by a relative error of at most 0.009.
Values may be sent and summed in bfloat16 or wider, within the bound.
A program may use at most 128 MiB of HBM per device.

v0:
```python
import math

import jax
import jax.numpy as jnp
from jax import lax
from jax.sharding import PartitionSpec as P

HEADS = 8
HEAD_DIM = 64
RADIUS = 6
CONV_RADIUS = 3
LAYERS = 2


def with_halo(shard, sides, width, wrap):
    for axis, dim in sides:
        peers, length = (lax.axis_size(axis), shard.shape[dim])
        up = [(i, (i + 1) % peers) for i in range(peers if wrap else peers - 1)]
        down = [(j, i) for i, j in up]
        last = lax.slice_in_dim(shard, length - width, length, axis=dim)
        leading = lax.slice_in_dim(shard, 0, width, axis=dim)
        before = lax.ppermute(last, axis, up)
        after = lax.ppermute(leading, axis, down)
        shard = jnp.concatenate([before, shard, after], axis=dim)
    return shard


def normalize(stream, gain):
    average = jnp.mean(stream, axis=-1, keepdims=True)
    centred = stream - average
    spread = jnp.mean(centred * centred, axis=-1, keepdims=True)
    return (centred * lax.rsqrt(spread + 1e-05) * gain).astype(jnp.bfloat16)


def attend_tile(queries, pairs, band_index, grid_height):
    tile_height, tile_width, channels = queries.shape
    side = 8
    span = side + 2 * RADIUS
    blocks_lat = tile_height // side
    blocks_lon = tile_width // side
    scale = 1.0 / math.sqrt(HEAD_DIM)
    query_rows = jnp.arange(side, dtype=jnp.int32)
    key_rows = jnp.arange(span, dtype=jnp.int32)
    near_local = jnp.abs(key_rows[None, :] - RADIUS - query_rows[:, None]) <= RADIUS
    anchor = jnp.zeros((), jnp.int32)

    def one_block(index):
        block_lat = index // blocks_lon
        block_lon = index % blocks_lon
        row_start = block_lat * side
        col_start = block_lon * side
        query_block = lax.dynamic_slice(
            queries, (row_start, col_start, anchor), (side, side, channels)
        )
        query_block = query_block.reshape(side * side, HEADS, HEAD_DIM)
        window = lax.dynamic_slice(
            pairs, (row_start, col_start, anchor), (span, span, 2 * channels)
        )
        window = window.reshape(span * span, 2 * channels)
        key_block = window[:, :channels].reshape(span * span, HEADS, HEAD_DIM)
        value_block = window[:, channels:].reshape(span * span, HEADS, HEAD_DIM)
        global_rows = band_index * tile_height + row_start + key_rows - RADIUS
        inside = (global_rows >= 0) & (global_rows < grid_height)
        near_rows = near_local & inside[None, :]
        allowed = near_rows[:, None, :, None] & near_local[None, :, None, :]
        allowed = allowed.reshape(side * side, span * span)
        scores = (
            jnp.einsum("qhd,khd->hqk", query_block, key_block, preferred_element_type=jnp.float32)
            * scale
        )
        scores = jnp.where(allowed[None], scores, -jnp.inf)
        peak = jnp.max(scores, axis=-1, keepdims=True)
        expos = jnp.exp(scores - peak)
        weights = (expos / jnp.sum(expos, axis=-1, keepdims=True)).astype(jnp.bfloat16)
        mixed = jnp.einsum("hqk,khd->qhd", weights, value_block, preferred_element_type=jnp.float32)
        return mixed.astype(jnp.bfloat16).reshape(side * side, channels)

    outputs = lax.map(one_block, jnp.arange(blocks_lat * blocks_lon, dtype=jnp.int32))
    outputs = outputs.reshape(blocks_lat, blocks_lon, side, side, channels)
    outputs = jnp.transpose(outputs, (0, 2, 1, 3, 4))
    return outputs.reshape(tile_height * tile_width, channels)


def convolve_tile(wide, kernel, tile_height, tile_width):
    total = jnp.zeros((tile_height, tile_width, wide.shape[2]), jnp.float32)
    for down_shift in range(2 * CONV_RADIUS + 1):
        for east_shift in range(2 * CONV_RADIUS + 1):
            piece = wide[
                down_shift : down_shift + tile_height, east_shift : east_shift + tile_width
            ]
            total = total + piece.astype(jnp.float32) * kernel[down_shift, east_shift].astype(
                jnp.float32
            )
    return total


def per_device(
    state,
    attention_in,
    attention_out,
    expand_weight,
    depth_kernel,
    shrink_weight,
    norm_attention,
    norm_feedforward,
):
    tile_height, tile_width, channels = state.shape
    band_index = lax.axis_index("lat")
    grid_height = tile_height * lax.axis_size("lat")
    extent_attention = (tile_height + 2 * RADIUS, tile_width + 2 * RADIUS, 2 * channels)
    stream = state.astype(jnp.float32).reshape(tile_height * tile_width, channels)
    for layer in range(LAYERS):
        normed = normalize(stream, norm_attention[layer])
        weight_in = attention_in[layer]
        queries = jnp.dot(
            normed, weight_in[:, :channels], preferred_element_type=jnp.float32
        ).astype(jnp.bfloat16)
        widened = normed.reshape(tile_height, tile_width, channels)
        widened = with_halo(widened, (("lat", 0),), RADIUS, False)
        widened = with_halo(widened, (("lon", 1),), RADIUS, True)
        pairs = jnp.dot(
            widened.reshape(-1, channels),
            weight_in[:, channels:],
            preferred_element_type=jnp.float32,
        ).astype(jnp.bfloat16)
        pairs = pairs.reshape(extent_attention)
        mixed = attend_tile(
            queries.reshape(tile_height, tile_width, channels), pairs, band_index, grid_height
        )
        stream = stream + jnp.dot(mixed, attention_out[layer], preferred_element_type=jnp.float32)
        normed_ff = normalize(stream, norm_feedforward[layer])
        hidden = jnp.dot(
            normed_ff, expand_weight[layer], preferred_element_type=jnp.float32
        ).astype(jnp.bfloat16)
        hidden = hidden.reshape(tile_height, tile_width, -1)
        hidden = with_halo(hidden, (("lat", 0),), CONV_RADIUS, False)
        hidden = with_halo(hidden, (("lon", 1),), CONV_RADIUS, True)
        convolved = convolve_tile(hidden, depth_kernel[layer], tile_height, tile_width)
        activated = (
            jax.nn.gelu(convolved, approximate=False)
            .astype(jnp.bfloat16)
            .reshape(tile_height * tile_width, -1)
        )
        stream = stream + jnp.dot(
            activated, shrink_weight[layer], preferred_element_type=jnp.float32
        )
    return stream.astype(jnp.bfloat16).reshape(tile_height, tile_width, channels)


def solution(mesh):
    in_specs = (P("lat", "lon", None), P(), P(), P(), P(), P(), P(), P())
    out_specs = P("lat", "lon", None)
    return jax.shard_map(
        per_device, mesh=mesh, in_specs=in_specs, out_specs=out_specs, check_vma=False
    )
```

profile of v0, /device:TPU:0, one launch (start us, length us, event | category | flops | bytes accessed | tf_op | source)
XLA Modules:
  0.0 826.8 jit_solution(5828780813669611630)
XLA Ops:
  4.3 1.8 fusion.61
  7.0 4.9 collective-permute-start
  15.0 1.9 slice_bitcast_fusion
  16.9 1.8 fusion.96
  19.8 2.8 convolution_convert_fusion.7
  22.6 4.1 collective-permute-done.1
  27.7 4.0 collective-permute-start.3
  32.3 3.9 collective-permute-done.2
  36.2 2.4 pad_maximum_fusion.6
  38.6 2.0 reshape.311
  40.6 6.4 convolution_convert_fusion.5
  47.1 6.1 reshape.312
  54.3 157.6 %while.28 = (s32[]{:T(128)}, bf16[18,64,512]{2,1,0:T(8,128)(2,1)}, s32[18]{0:T(128)S(1)}, bf16[36,60,1024]{2,1,0:T(8,128)(2,1)}, s32[]{:T(128)}, /*index=5*/bf16...) while((s32[]{:T(128)}, bf16[18,64,512]{2,1,0:T(8,128)(2,1)}, ...), condition=%wide.region_5.6_spmd.clone.clone, body=%wide.region_2.5_spmd.clone.clone.sunk | while | flops 80546848 | bytes 10275530 | solution.py:78
  65.4 1.8 constant_dynamic-slice_fusion.8
  74.2 1.8 constant_dynamic-slice_fusion.8
  83.0 1.8 constant_dynamic-slice_fusion.8
  109.2 1.8 constant_dynamic-slice_fusion.8
  213.5 2.0 fusion.99
  216.0 3.2 convolution_convert_fusion.3
  219.3 3.4 collective-permute-start.4
  225.6 9.4 %collective-permute-done.4 = bf16[3,48,2048]{2,1,0:T(8,128)(2,1)S(1)} collective-permute-done((bf16[3,48,2048]{2,1,0:T(8,128)(2,1)S(1)}, bf16[3,48,2048]{2,1,0:T(8,128)(2,1)S(1)}, u32[]{:S(2)}, u32[]{:S(2)}) %collective-permute-start.4) | collective-permute-done | bytes 589856 | tf_op jit(solution)/shard_map/ppermute | solution.py:22
  235.0 12.8 %collective-permute-done.5 = bf16[3,48,2048]{2,1,0:T(8,128)(2,1)S(1)} collective-permute-done((bf16[3,48,2048]{2,1,0:T(8,128)(2,1)S(1)}, bf16[3,48,2048]{2,1,0:T(8,128)(2,1)S(1)}, u32[]{:S(2)}, u32[]{:S(2)}) %collective-permute-start.5) | collective-permute-done | bytes 589856 | tf_op jit(solution)/shard_map/ppermute | solution.py:23
  249.9 2.5 collective-permute-start.7
  253.2 7.4 collective-permute-done.6
  260.6 2.6 collective-permute-done.7
  263.2 6.6 maximum_maximum_fusion
  269.8 146.3 %fusion.32 = bf16[24,48,2048]{2,1,0:T(8,128)(2,1)} fusion(bf16[24,48,2048]{2,1,0:T(8,128)(2,1)} %bitcast.248, bf16[3,48,2048]{2,1,0:T(8,128)(2,1)S(1)} %collective-permute-done.5, bf16[3,48,2048]{2,1,0:T(8,128)(2,1)S(1)} %collective-permute-done.4, bf16[30,51,2048]{2,1,0:T(8,128)(2,1)} %get-tuple-element.358, bf16[30,51,2048]{2,1,0:T(8,128)(2,1)} %get-tuple-element.357, ...), kind=kLoop, calls=%fused_computation.48 | loop fusion | flops 511967232 | bytes 209199104 | tf_op jit(solution)/shard_map/convert_element_type | solution.py:141
  416.1 5.8 fusion.100
  423.8 2.8 collective-permute-start.8
  427.8 5.7 collective-permute-done.8
  433.5 7.1 collective-permute-done.9
  440.8 3.7 collective-permute-start.11
  444.5 2.8 convolution_convert_fusion.6
  447.3 4.1 collective-permute-done.10
  451.5 2.4 pad_maximum_fusion.7
  453.9 2.0 reshape.319
  455.9 6.4 convolution_convert_fusion.4
  462.4 6.1 reshape.320
  468.6 150.0 %while.29 = (s32[]{:T(128)}, bf16[18,64,512]{2,1,0:T(8,128)(2,1)S(1)}, s32[18]{0:T(128)S(1)}, bf16[36,60,1024]{2,1,0:T(8,128)(2,1)}, s32[]{:T(128)}, /*index=5*/...) while((s32[]{:T(128)}, ...), condition=%wide.region_13.14_spmd.clone.clone, body=%wide.region_10.13_spmd.clone.clone.sunk | while | flops 80546848 | bytes 10275022 | solution.py:78
  618.8 2.8 fusion.101
  622.1 3.2 convolution_convert_fusion.2
  630.0 9.3 %collective-permute-done.12 = bf16[3,48,2048]{2,1,0:T(8,128)(2,1)S(1)} collective-permute-done((bf16[3,48,2048]{2,1,0:T(8,128)(2,1)S(1)}, bf16[3,48,2048]{2,1,0:T(8,128)(2,1)S(1)}, u32[]{:S(2)}, u32[]{:S(2)}) %collective-permute-start.12) | collective-permute-done | bytes 589856 | tf_op jit(solution)/shard_map/ppermute | solution.py:22
  639.3 13.2 %collective-permute-done.13 = bf16[3,48,2048]{2,1,0:T(8,128)(2,1)S(1)} collective-permute-done((bf16[3,48,2048]{2,1,0:T(8,128)(2,1)S(1)}, bf16[3,48,2048]{2,1,0:T(8,128)(2,1)S(1)}, u32[]{:S(2)}, u32[]{:S(2)}) %collective-permute-start.13) | collective-permute-done | bytes 589856 | tf_op jit(solution)/shard_map/ppermute | solution.py:23
  653.2 3.8 collective-permute-start.15
  657.6 9.3 %collective-permute-done.14 = bf16[30,3,2048]{2,1,0:T(4,128)(2,1)S(1)} collective-permute-done((bf16[30,3,2048]{2,1,0:T(4,128)(2,1)S(1)}, bf16[30,3,2048]{2,1,0:T(4,128)(2,1)S(1)}, u32[]{:S(2)}, u32[]{:S(2)}) %collective-permute-start.14) | collective-permute-done | bytes 368672 | tf_op jit(solution)/shard_map/ppermute | solution.py:22
  666.9 6.6 maximum_maximum_fusion.1
  673.5 146.4 %fusion.35 = bf16[24,48,2048]{2,1,0:T(8,128)(2,1)} fusion(bf16[24,48,2048]{2,1,0:T(8,128)(2,1)} %bitcast.245, bf16[3,48,2048]{2,1,0:T(8,128)(2,1)S(1)} %collective-permute-done.13, bf16[3,48,2048]{2,1,0:T(8,128)(2,1)S(1)} %collective-permute-done.12, bf16[30,51,2048]{2,1,0:T(8,128)(2,1)} %get-tuple-element.354, bf16[30,51,2048]{2,1,0:T(8,128)(2,1)} %get-tuple-element.353, ...), kind=kLoop, calls=%fused_computation.51 | loop fusion | flops 511967232 | bytes 209199104 | tf_op jit(solution)/shard_map/convert_element_type | solution.py:141
  819.9 6.7 fusion.58
  (696 shorter events, 260.3 us)
Async XLA Ops:
  3.4 11.5 %copy-start.6 = (bf16[2,512,1536]{2,1,0:T(8,128)(2,1)S(1)}, bf16[2,512,1536]{2,1,0:T(8,128)(2,1)}, u32[]{:S(2)}) copy-start(bf16[2,512,1536]{2,1,0:T(8,128)(2,1)} %param.13) | copy-start | bytes 9437188
  7.0 15.6 %collective-permute-start = (bf16[6,48,512]{2,1,0:T(8,128)(2,1)}, bf16[6,48,512]{2,1,0:T(8,128)(2,1)S(1)}, u32[]{:S(2)}, u32[]{:S(2)}) collective-permute-start(bf16[6,48,512]{2,1,0:T(8,128)(2,1)} %bitcast.2), channel_id=1, source_target_pairs={{0,1},{1,2},{2,3},{4,5},{5,6},{6,7},{8,9},{9,10},{10,11},{12,13},{... | collective-permute-start | bytes 884744 | tf_op jit(solution)/shard_map/ppermute | solution.py:22
  11.9 14.8 %collective-permute-start.1 = (bf16[6,48,512]{2,1,0:T(8,128)(2,1)}, bf16[6,48,512]{2,1,0:T(8,128)(2,1)}, u32[]{:S(2)}, u32[]{:S(2)}) collective-permute-start(bf16[6,48,512]{2,1,0:T(8,128)(2,1)} %bitcast.3), channel_id=1, source_target_pairs={{1,0},{2,1},{3,2},{5,4},{6,5},{7,6},{9,8},{10,9},{11,10},{13,12},{... | collective-permute-start | bytes 884744 | tf_op jit(solution)/shard_map/ppermute | solution.py:23
  15.0 16.8 %copy-start.12 = (f32[2,512]{1,0:T(2,128)S(1)}, f32[2,512]{1,0:T(2,128)}, u32[]{:S(2)}) copy-start(f32[2,512]{1,0:T(2,128)} %param.19) | copy-start | bytes 12292
  22.6 13.5 %copy-start.9 = (bf16[6,48,512]{2,1,0:T(8,128)(2,1)}, bf16[6,48,512]{2,1,0:T(8,128)(2,1)S(1)}, u32[]{:S(2)}) copy-start(bf16[6,48,512]{2,1,0:T(8,128)(2,1)S(1)} %collective-permute-done) | copy-start | bytes 884740
  27.6 8.6 %collective-permute-start.2 = (bf16[36,6,512]{2,1,0:T(8,128)(2,1)S(1)}, bf16[36,6,512]{2,1,0:T(8,128)(2,1)S(1)}, u32[]{:S(2)}, u32[]{:S(2)}) collective-permute-start(bf16[36,6,512]{2,1,0:T(8,128)(2,1)S(1)} %get-tuple-element.369), channel_id=1, source_target_pairs={{0,4},{4,8},{8,12},{12,16},{16,20},{20,24},{24,28},{28,0},{1,5},{5... | collective-permute-start | bytes 663560 | tf_op jit(solution)/shard_map/ppermute | solution.py:22
  27.7 8.5 %collective-permute-start.3 = (bf16[36,6,512]{2,1,0:T(8,128)(2,1)S(1)}, bf16[36,6,512]{2,1,0:T(8,128)(2,1)S(1)}, u32[]{:S(2)}, u32[]{:S(2)}) collective-permute-start(bf16[36,6,512]{2,1,0:T(8,128)(2,1)S(1)} %get-tuple-element.370), channel_id=1, source_target_pairs={{4,0},{8,4},{12,8},{16,12},{20,16},{24,20},{28,24},{0,28},{5,1},{9... | collective-permute-start | bytes 663560 | tf_op jit(solution)/shard_map/ppermute | solution.py:23
  54.3 159.1 %copy-start.2 = (bf16[24,48,512]{2,1,0:T(8,128)(2,1)S(1)}, bf16[24,48,512]{2,1,0:T(8,128)(2,1)}, u32[]{:S(2)}) copy-start(bf16[24,48,512]{2,1,0:T(8,128)(2,1)} %param.12) | copy-start | bytes 3538948
  211.9 4.1 copy-start.14
  211.9 4.1 copy-start.15
  215.5 3.7 copy-start.4
  216.0 8.1 copy-start.8
  219.2 50.6 %copy-start.1 = (bf16[1152,2048]{1,0:T(8,128)(2,1)}, bf16[1152,2048]{1,0:T(8,128)(2,1)S(1)}, u32[]{:S(2)}) copy-start(bf16[1152,2048]{1,0:T(8,128)(2,1)S(1)} %convolution_convert_fusion.3) | copy-start | bytes 14155780
  219.3 15.7 %collective-permute-start.4 = (bf16[3,48,2048]{2,1,0:T(8,128)(2,1)S(1)}, bf16[3,48,2048]{2,1,0:T(8,128)(2,1)S(1)}, u32[]{:S(2)}, u32[]{:S(2)}) collective-permute-start(bf16[3,48,2048]{2,1,0:T(8,128)(2,1)S(1)} %bitcast.265), channel_id=1, source_target_pairs={{0,1},{1,2},{2,3},{4,5},{5,6},{6,7},{8,9},{9,10},{10,11},{12,13},{... | collective-permute-start | bytes 1769480 | tf_op jit(solution)/shard_map/ppermute | solution.py:22
  222.7 25.0 %collective-permute-start.5 = (bf16[3,48,2048]{2,1,0:T(8,128)(2,1)S(1)}, bf16[3,48,2048]{2,1,0:T(8,128)(2,1)S(1)}, u32[]{:S(2)}, u32[]{:S(2)}) collective-permute-start(bf16[3,48,2048]{2,1,0:T(8,128)(2,1)S(1)} %bitcast.263), channel_id=1, source_target_pairs={{1,0},{2,1},{3,2},{5,4},{6,5},{7,6},{9,8},{10,9},{11,10},{13,12},{... | collective-permute-start | bytes 1769480 | tf_op jit(solution)/shard_map/ppermute | solution.py:23
  248.3 12.2 %collective-permute-start.6 = (bf16[30,3,2048]{2,1,0:T(4,128)(2,1)S(1)}, bf16[30,3,2048]{2,1,0:T(4,128)(2,1)S(1)}, u32[]{:S(2)}, u32[]{:S(2)}) collective-permute-start(bf16[30,3,2048]{2,1,0:T(4,128)(2,1)S(1)} %get-tuple-element.359), channel_id=1, source_target_pairs={{0,4},{4,8},{8,12},{12,16},{16,20},{20,24},{24,28},{28,0},{1,5},{5... | collective-permute-start | bytes 1105928 | tf_op jit(solution)/shard_map/ppermute | solution.py:22
  249.9 13.2 %collective-permute-start.7 = (bf16[30,3,2048]{2,1,0:T(4,128)(2,1)S(1)}, bf16[30,3,2048]{2,1,0:T(4,128)(2,1)S(1)}, u32[]{:S(2)}, u32[]{:S(2)}) collective-permute-start(bf16[30,3,2048]{2,1,0:T(4,128)(2,1)S(1)} %get-tuple-element.360), channel_id=1, source_target_pairs={{4,0},{8,4},{12,8},{16,12},{20,16},{24,20},{28,24},{0,28},{5,1},{9... | collective-permute-start | bytes 1105928 | tf_op jit(solution)/shard_map/ppermute | solution.py:23
  269.8 146.3 %copy-start.5 = (f32[1152,512]{1,0:T(8,128)S(1)}, f32[1152,512]{1,0:T(8,128)}, u32[]{:S(2)}) copy-start(f32[1152,512]{1,0:T(8,128)} %copy-done.4) | copy-start | bytes 7077892
  421.9 1.4 copy-start.3
  423.8 9.8 %collective-permute-start.8 = (bf16[6,48,512]{2,1,0:T(8,128)(2,1)S(1)}, bf16[6,48,512]{2,1,0:T(8,128)(2,1)S(1)}, u32[]{:S(2)}, u32[]{:S(2)}) collective-permute-start(bf16[6,48,512]{2,1,0:T(8,128)(2,1)S(1)} %bitcast.267), channel_id=1, source_target_pairs={{0,1},{1,2},{2,3},{4,5},{5,6},{6,7},{8,9},{9,10},{10,11},{12,13},{... | collective-permute-start | bytes 884744 | tf_op jit(solution)/shard_map/ppermute | solution.py:22
  426.5 14.1 %collective-permute-start.9 = (bf16[6,48,512]{2,1,0:T(8,128)(2,1)S(1)}, bf16[6,48,512]{2,1,0:T(8,128)(2,1)S(1)}, u32[]{:S(2)}, u32[]{:S(2)}) collective-permute-start(bf16[6,48,512]{2,1,0:T(8,128)(2,1)S(1)} %bitcast.266), channel_id=1, source_target_pairs={{1,0},{2,1},{3,2},{5,4},{6,5},{7,6},{9,8},{10,9},{11,10},{13,12},{... | collective-permute-start | bytes 884744 | tf_op jit(solution)/shard_map/ppermute | solution.py:23
  433.5 17.9 %copy-start.10 = (bf16[6,48,512]{2,1,0:T(8,128)(2,1)}, bf16[6,48,512]{2,1,0:T(8,128)(2,1)S(1)}, u32[]{:S(2)}) copy-start(bf16[6,48,512]{2,1,0:T(8,128)(2,1)S(1)} %collective-permute-done.8) | copy-start | bytes 884740
  440.6 10.8 %copy-start.11 = (bf16[6,48,512]{2,1,0:T(8,128)(2,1)}, bf16[6,48,512]{2,1,0:T(8,128)(2,1)S(1)}, u32[]{:S(2)}) copy-start(bf16[6,48,512]{2,1,0:T(8,128)(2,1)S(1)} %collective-permute-done.9) | copy-start | bytes 884740
  440.7 10.7 %collective-permute-start.10 = (bf16[36,6,512]{2,1,0:T(8,128)(2,1)S(1)}, bf16[36,6,512]{2,1,0:T(8,128)(2,1)S(1)}, u32[]{:S(2)}, u32[]{:S(2)}) collective-permute-start(bf16[36,6,512]{2,1,0:T(8,128)(2,1)S(1)} %get-tuple-element.367), channel_id=1, source_target_pairs={{0,4},{4,8},{8,12},{12,16},{16,20},{20,24},{24,28},{28,0},{1,5},{5... | collective-permute-start | bytes 663560 | tf_op jit(solution)/shard_map/ppermute | solution.py:22
  440.8 10.6 %collective-permute-start.11 = (bf16[36,6,512]{2,1,0:T(8,128)(2,1)S(1)}, bf16[36,6,512]{2,1,0:T(8,128)(2,1)S(1)}, u32[]{:S(2)}, u32[]{:S(2)}) collective-permute-start(bf16[36,6,512]{2,1,0:T(8,128)(2,1)S(1)} %get-tuple-element.368), channel_id=1, source_target_pairs={{4,0},{8,4},{12,8},{16,12},{20,16},{24,20},{28,24},{0,28},{5,1},{9... | collective-permute-start | bytes 663560 | tf_op jit(solution)/shard_map/ppermute | solution.py:23
  618.6 3.5 copy-start.13
  618.6 3.5 copy-start.16
  622.1 6.4 copy-start.7
  625.3 48.2 %copy-start = (bf16[1152,2048]{1,0:T(8,128)(2,1)}, bf16[1152,2048]{1,0:T(8,128)(2,1)S(1)}, u32[]{:S(2)}) copy-start(bf16[1152,2048]{1,0:T(8,128)(2,1)S(1)} %convolution_convert_fusion.2) | copy-start | bytes 14155780
  625.4 13.9 %collective-permute-start.12 = (bf16[3,48,2048]{2,1,0:T(8,128)(2,1)S(1)}, bf16[3,48,2048]{2,1,0:T(8,128)(2,1)S(1)}, u32[]{:S(2)}, u32[]{:S(2)}) collective-permute-start(bf16[3,48,2048]{2,1,0:T(8,128)(2,1)S(1)} %bitcast.264), channel_id=1, source_target_pairs={{0,1},{1,2},{2,3},{4,5},{5,6},{6,7},{8,9},{9,10},{10,11},{12,13},{... | collective-permute-start | bytes 1769480 | tf_op jit(solution)/shard_map/ppermute | solution.py:22
  627.2 25.4 %collective-permute-start.13 = (bf16[3,48,2048]{2,1,0:T(8,128)(2,1)S(1)}, bf16[3,48,2048]{2,1,0:T(8,128)(2,1)S(1)}, u32[]{:S(2)}, u32[]{:S(2)}) collective-permute-start(bf16[3,48,2048]{2,1,0:T(8,128)(2,1)S(1)} %bitcast.262), channel_id=1, source_target_pairs={{1,0},{2,1},{3,2},{5,4},{6,5},{7,6},{9,8},{10,9},{11,10},{13,12},{... | collective-permute-start | bytes 1769480 | tf_op jit(solution)/shard_map/ppermute | solution.py:23
  653.1 13.8 %collective-permute-start.14 = (bf16[30,3,2048]{2,1,0:T(4,128)(2,1)S(1)}, bf16[30,3,2048]{2,1,0:T(4,128)(2,1)S(1)}, u32[]{:S(2)}, u32[]{:S(2)}) collective-permute-start(bf16[30,3,2048]{2,1,0:T(4,128)(2,1)S(1)} %get-tuple-element.355), channel_id=1, source_target_pairs={{0,4},{4,8},{8,12},{12,16},{16,20},{20,24},{24,28},{28,0},{1,5},{5... | collective-permute-start | bytes 1105928 | tf_op jit(solution)/shard_map/ppermute | solution.py:22
  653.2 13.7 %collective-permute-start.15 = (bf16[30,3,2048]{2,1,0:T(4,128)(2,1)S(1)}, bf16[30,3,2048]{2,1,0:T(4,128)(2,1)S(1)}, u32[]{:S(2)}, u32[]{:S(2)}) collective-permute-start(bf16[30,3,2048]{2,1,0:T(4,128)(2,1)S(1)} %get-tuple-element.356), channel_id=1, source_target_pairs={{4,0},{8,4},{12,8},{16,12},{20,16},{24,20},{28,24},{0,28},{5,1},{9... | collective-permute-start | bytes 1105928 | tf_op jit(solution)/shard_map/ppermute | solution.py:23
where the time goes:
time: 835 us; the launch traced here: 827 us
  other arithmetic  332 us (40%)
  local copies, waits for them, and re-layouts  196 us (23%)
  matrix products  105 us (13%)
  waiting for transfers between devices  88.9 us (11%)
  loops' own time  69.9 us (8%)
  starting transfers between devices  33.8 us (4%)
    convert_element_type x2, other arithmetic, per_device(): activated = jax.nn.gelu(convolved, approximate=False).astype(jnp.bfloat16...  293 us
    another operation x2, loops' own time, attend_tile(): lax.map(one_block, jnp.arange(blocks_lat * blocks_lon, dtype=jnp.int32))  69.9 us
    dynamic_slice x36, local copies, waits for them, and re-layouts, one_block(): lax.dynamic_slice(pairs, (row_start, col_start, anchor), (span, span, 2 *...  62.8 us
    ppermute x8, waiting for transfers between devices, with_halo(): before = lax.ppermute(last, axis, up)  49.1 us
    ppermute x8, waiting for transfers between devices, with_halo(): after = lax.ppermute(leading, axis, down)  39.8 us
    dot_general x36, matrix products, one_block(): jnp.einsum('hqk,khd->qhd', weights, value_block, preferred_element_type=j...  35.4 us
    dynamic_slice x36, local copies, waits for them, and re-layouts, one_block(): lax.dynamic_slice(queries, (row_start, col_start, anchor), (side, side, c...  30.6 us
    dynamic_slice x36, local copies, waits for them, and re-layouts, attend_tile(): lax.map(one_block, jnp.arange(blocks_lat * blocks_lon, dtype=jnp.int32))  21 us
  transfers between devices with their start and end apart: 16, of which 12 were waited for; matrix products, arithmetic and copies ran while one was open for 2% of the time, Pallas kernels for 0%

commit v1 on v0

v1 whole, which is shorter than its diff:
```python
import functools
import math

import jax
import jax.numpy as jnp
import numpy as np
from jax import lax
from jax.experimental import pallas as pl
from jax.experimental.pallas import tpu as pltpu
from jax.sharding import PartitionSpec as P

HEADS = 8
HEAD_DIM = 64
RADIUS = 6
CONV_RADIUS = 3
LAYERS = 2
Q_LAT = 4
Q_LON = 16
K_LAT = Q_LAT + 2 * RADIUS
K_LON = 32
GROUP = 4
NEG = -1e30
VMEM_LIMIT = 60 * 1024 * 1024
F32 = jnp.float32
BF16 = jnp.bfloat16


def with_halo(shard, sides, width, wrap):
    for axis, dim in sides:
        peers, length = (lax.axis_size(axis), shard.shape[dim])
        up = [(i, (i + 1) % peers) for i in range(peers if wrap else peers - 1)]
        down = [(j, i) for i, j in up]
        last = lax.slice_in_dim(shard, length - width, length, axis=dim)
        leading = lax.slice_in_dim(shard, 0, width, axis=dim)
        before = lax.ppermute(last, axis, up)
        after = lax.ppermute(leading, axis, down)
        parts = [before, shard, after]
        if dim == 1:
            extra = -(length + 2 * width) % 16
            parts.append(jnp.zeros((shard.shape[0], extra, shard.shape[2]), shard.dtype))
        shard = jnp.concatenate(parts, axis=dim)
    return shard


def halo(tile, width):
    tile = with_halo(tile, (("lat", 0),), width, False)
    return with_halo(tile, (("lon", 1),), width, True)


def norm_rows(stream, gain):
    average = jnp.mean(stream, axis=-1, keepdims=True)
    centred = stream - average
    spread = jnp.mean(centred * centred, axis=-1, keepdims=True)
    return (centred * lax.rsqrt(spread + 1e-05) * gain).astype(BF16)


def erf(x):
    x = jnp.clip(x, -3.832506856900711, 3.832506856900711)
    s = x * x
    a = (
        0.00022905065861350646,
        0.0034082910107109506,
        0.050955695062380861,
        0.18520832239976145,
        1.128379143519084,
    )
    b = (
        -1.1791602954361697e-7,
        0.000023547966471313185,
        0.0010179625278914885,
        0.014070470171167667,
        0.11098505178285362,
        0.49746925110067538,
        1.0,
    )
    top = jnp.full_like(x, a[0])
    for value in a[1:]:
        top = top * s + value
    low = jnp.full_like(x, b[0])
    for value in b[1:]:
        low = low * s + value
    return x * top / low


def gelu(x):
    return 0.5 * x * (1.0 + lax.erf(x * math.sqrt(0.5)))


def attention_kernel(
    own_ref, ext_ref, win_ref, wout_ref, bias_ref, stream_ref, gain_ref,
    out_ref, normed_ref, q_ref, kv_ref, mixed_ref,
):
    height, width, channels = own_ref.shape
    rows, wide, _ = ext_ref.shape
    span = GROUP * HEAD_DIM
    part = Q_LAT * Q_LON

    @pl.loop(0, rows // 4)
    def _(r):
        x = ext_ref[pl.ds(r * 4, 4)].reshape(4 * wide, channels)
        y = jnp.dot(x, win_ref[:, channels:], preferred_element_type=F32)
        kv_ref[pl.ds(r * 4, 4)] = y.astype(BF16).reshape(4, wide, 2 * channels)

    @pl.loop(0, height // 4)
    def _(r):
        x = own_ref[pl.ds(r * 4, 4)].reshape(4 * width, channels)
        y = jnp.dot(x, win_ref[:, :channels], preferred_element_type=F32)
        y = y.astype(BF16) * (1.0 / math.sqrt(HEAD_DIM))
        q_ref[pl.ds(r * 4, 4)] = y.astype(BF16).reshape(4, width, channels)

    lane_head = lax.broadcasted_iota(jnp.int32, (part, span), 1) // HEAD_DIM

    def block(index, carry):
        lat = index // (width // Q_LON)
        lon = index % (width // Q_LON)
        r0 = lat * Q_LAT
        c0 = pl.multiple_of(lon * Q_LON, Q_LON)
        bias = bias_ref[lat]
        for g in range(channels // span):
            lo = g * span
            q = q_ref[pl.ds(r0, Q_LAT), pl.ds(c0, Q_LON), lo : lo + span].reshape(part, span)
            k = kv_ref[pl.ds(r0, K_LAT), pl.ds(c0, K_LON), lo : lo + span]
            v = kv_ref[
                pl.ds(r0, K_LAT), pl.ds(c0, K_LON), channels + lo : channels + lo + span
            ]
            k = k.reshape(K_LAT * K_LON, span)
            v = v.reshape(K_LAT * K_LON, span)
            qq = jnp.concatenate(
                [jnp.where(lane_head == h, q, jnp.zeros_like(q)) for h in range(GROUP)], axis=0
            )
            s = lax.dot_general(qq, k, (((1,), (1,)), ((), ())), preferred_element_type=F32)
            s = (s.reshape(GROUP, part, K_LAT * K_LON) + bias[None]).reshape(s.shape)
            peak = jnp.max(s, axis=-1, keepdims=True)
            e = jnp.exp(s - peak)
            total = jnp.sum(e, axis=-1, keepdims=True)
            o = jnp.dot(e.astype(BF16), v, preferred_element_type=F32) * (1.0 / total)
            m = jnp.zeros((part, span), F32)
            for h in range(GROUP):
                m = jnp.where(lane_head == h, o[h * part : (h + 1) * part], m)
            mixed_ref[pl.ds(r0, Q_LAT), pl.ds(c0, Q_LON), lo : lo + span] = m.astype(
                BF16
            ).reshape(Q_LAT, Q_LON, span)
        return carry

    lax.fori_loop(0, (height // Q_LAT) * (width // Q_LON), block, 0)

    @pl.loop(0, height // 4)
    def _(r):
        x = mixed_ref[pl.ds(r * 4, 4)].reshape(4 * width, channels)
        y = jnp.dot(x, wout_ref[...], preferred_element_type=F32)
        y = y + stream_ref[pl.ds(r * 4, 4)].reshape(4 * width, channels)
        out_ref[pl.ds(r * 4, 4)] = y.reshape(4, width, channels)
        normed_ref[pl.ds(r * 4, 4)] = norm_rows(y, gain_ref[...]).reshape(4, width, channels)


def feed_kernel(last, ext_ref, expand_ref, taps_ref, shrink_ref, stream_ref, gain_ref, *refs):
    if last:
        out_ref, hid_ref, act_ref, acc_ref = refs
    else:
        out_ref, normed_ref, hid_ref, act_ref, acc_ref = refs
    height, width, channels = stream_ref.shape
    rows, wide, _ = ext_ref.shape
    chunk = expand_ref.shape[1]
    side = 2 * CONV_RADIUS + 1
    step = pl.program_id(0)

    @pl.loop(0, rows // 5)
    def _(r):
        x = ext_ref[pl.ds(r * 5, 5)].reshape(5 * wide, channels)
        y = jnp.dot(x, expand_ref[...], preferred_element_type=F32)
        hid_ref[pl.ds(r * 5, 5)] = y.astype(BF16).reshape(5, wide, chunk)

    parts = chunk // 128

    def conv_row(n, carry):
        i = n // parts
        lanes = pl.ds(pl.multiple_of((n % parts) * 128, 128), 128)
        lines = [hid_ref[i + a, :, lanes].reshape(wide // 16, 16, 128) for a in range(side)]
        total = None
        for b in range(side):
            p = lines[0] * taps_ref[0, b, :, lanes]
            for a in range(1, side):
                p = p + lines[a] * taps_ref[a, b, :, lanes]
            p = p.reshape(wide, 128).astype(F32)[b : b + width]
            total = p if total is None else total + p
        act_ref[i, :, lanes] = gelu(total).astype(BF16)
        return carry

    lax.fori_loop(0, height * parts, conv_row, 0)

    @pl.loop(0, height // 4)
    def _(r):
        x = act_ref[pl.ds(r * 4, 4)].reshape(4 * width, chunk)
        y = jnp.dot(x, shrink_ref[...], preferred_element_type=F32)
        rs = pl.ds(r * 4, 4)

        @pl.when(step == 0)
        def _():
            acc_ref[rs] = stream_ref[rs] + y.reshape(4, width, channels)

        @pl.when(step > 0)
        def _():
            acc_ref[rs] = acc_ref[rs] + y.reshape(4, width, channels)

    @pl.when(step == pl.num_programs(0) - 1)
    def _():
        @pl.loop(0, height // 4)
        def _(r):
            rs = pl.ds(r * 4, 4)
            y = acc_ref[rs]
            out_ref[rs] = y.astype(out_ref.dtype)
            if not last:
                z = norm_rows(y.reshape(4 * width, channels), gain_ref[...])
                normed_ref[rs] = z.reshape(4, width, channels)


def full(shape):
    return pl.BlockSpec(shape, lambda *_: (0,) * len(shape))


def attention(own, ext, w_in, w_out, bias, stream, gain):
    shape = own.shape
    height, width, channels = shape
    args = (own, ext, w_in, w_out, bias, stream, gain)
    return pl.pallas_call(
        attention_kernel,
        out_shape=(jax.ShapeDtypeStruct(shape, F32), jax.ShapeDtypeStruct(shape, BF16)),
        in_specs=[pl.BlockSpec(memory_space=pltpu.VMEM)] * len(args),
        out_specs=(pl.BlockSpec(memory_space=pltpu.VMEM),) * 2,
        scratch_shapes=[
            pltpu.VMEM(shape, BF16),
            pltpu.VMEM(ext.shape[:2] + (2 * channels,), BF16),
            pltpu.VMEM(shape, BF16),
        ],
        compiler_params=pltpu.CompilerParams(vmem_limit_bytes=VMEM_LIMIT),
        name="attend",
    )(*args)


def feed(last, ext, expand, taps, shrink, stream, gain):
    shape = stream.shape
    height, width, channels = shape
    units = expand.shape[1]
    chunk = min(512, units)
    side = 2 * CONV_RADIUS + 1
    out_shape = [jax.ShapeDtypeStruct(shape, BF16 if last else F32)]
    if not last:
        out_shape.append(jax.ShapeDtypeStruct(shape, BF16))
    return pl.pallas_call(
        functools.partial(feed_kernel, last),
        out_shape=out_shape,
        grid=(units // chunk,),
        in_specs=[
            full(ext.shape),
            pl.BlockSpec((channels, chunk), lambda j: (0, j)),
            pl.BlockSpec((side, side, 16, chunk), lambda j: (0, 0, 0, j)),
            pl.BlockSpec((chunk, channels), lambda j: (j, 0)),
            full(shape),
            full(gain.shape),
        ],
        out_specs=[full(shape) for _ in out_shape],
        scratch_shapes=[
            pltpu.VMEM(ext.shape[:2] + (chunk,), BF16),
            pltpu.VMEM((height, width, chunk), BF16),
            pltpu.VMEM(shape, F32),
        ],
        compiler_params=pltpu.CompilerParams(vmem_limit_bytes=VMEM_LIMIT),
        name="feed",
    )(ext, expand, taps, shrink, stream, gain)


def score_bias(tile_height):
    band = lax.axis_index("lat")
    grid_height = tile_height * lax.axis_size("lat")
    qi, qj = np.arange(Q_LAT), np.arange(Q_LON)
    ki, kj = np.arange(K_LAT), np.arange(K_LON)
    near_lat = np.abs(ki[None, :] - RADIUS - qi[:, None]) <= RADIUS
    near_lon = np.abs(kj[None, :] - RADIUS - qj[:, None]) <= RADIUS
    starts = np.arange(tile_height // Q_LAT) * Q_LAT
    place = band * tile_height + starts[:, None] + ki[None, :] - RADIUS
    inside = (place >= 0) & (place < grid_height)
    ok_lat = near_lat[None] & inside[:, None, :]
    ok = ok_lat[:, :, None, :, None] & near_lon[None, None, :, None, :]
    bias = jnp.where(ok, 0.0, NEG).astype(F32)
    return bias.reshape(len(starts), Q_LAT * Q_LON, K_LAT * K_LON)


def per_device(
    state,
    attention_in,
    attention_out,
    expand_weight,
    depth_kernel,
    shrink_weight,
    norm_attention,
    norm_feedforward,
):
    bias = score_bias(state.shape[0])
    stream = state.astype(F32)
    normed = norm_rows(stream, norm_attention[0])
    for layer in range(LAYERS):
        last = layer == LAYERS - 1
        taps = depth_kernel[layer]
        taps = jnp.broadcast_to(taps[:, :, None, :], taps.shape[:2] + (16, taps.shape[2]))
        stream, normed_ff = attention(
            normed,
            halo(normed, RADIUS),
            attention_in[layer],
            attention_out[layer],
            bias,
            stream,
            norm_feedforward[layer][None],
        )
        outs = feed(
            last,
            halo(normed_ff, CONV_RADIUS),
            expand_weight[layer],
            taps,
            shrink_weight[layer],
            stream,
            norm_attention[min(layer + 1, LAYERS - 1)][None],
        )
        if last:
            return outs[0]
        stream, normed = outs


def solution(mesh):
    in_specs = (P("lat", "lon", None), P(), P(), P(), P(), P(), P(), P())
    out_specs = P("lat", "lon", None)
    return jax.shard_map(
        per_device, mesh=mesh, in_specs=in_specs, out_specs=out_specs, check_vma=False
    )
```

time: 835 us -> 329 us (0.39)
  other arithmetic: 332 us -> 18.6 us
  Pallas kernels: 0 us -> 206 us
  local copies, waits for them, and re-layouts: 196 us -> 27.3 us
  matrix products: 105 us -> 0 us
  loops' own time: 69.9 us -> 0 us
  waiting for transfers between devices: 88.9 us -> 40.5 us
    convert_element_type x5 -> x2, other arithmetic: 297 us -> 2.2 us  [the longest x1 1.76 us: per_device(): stream = state.astype(F32)]
    pallas_call x0 -> x4, Pallas kernels: none -> 206 us  [the longest x2 152 us: feed(): pl.pallas_call(functools.partial(feed_kernel, last), out_shape=out_shape,...]
    dynamic_slice x108 -> x0, local copies, waits for them, and re-layouts: 114 us -> none  [the longest x36 62.8 us: one_block(): lax.dynamic_slice(pairs, (row_start, col_start, anchor), (span, span, 2 *...]
    dot_general x82 -> x0, matrix products: 87.8 us -> none  [the longest x36 35.4 us: one_block(): jnp.einsum('hqk,khd->qhd', weights, value_block, preferred_element_type=j...]
    another operation x2 -> x0, loops' own time: 69.9 us -> none  [attend_tile(): lax.map(one_block, jnp.arange(blocks_lat * blocks_lon, dtype=jnp.int32))]
    reshape x76 -> x0, local copies, waits for them, and re-layouts: 26.9 us -> none  [the longest x2 12.2 us: per_device(): pairs = pairs.reshape(extent_attention)]
    ppermute x8, waiting for transfers between devices: 49.1 us -> 23.9 us  [with_halo(): before = lax.ppermute(last, axis, up)]
    ppermute x8, waiting for transfers between devices: 39.8 us -> 16.6 us  [with_halo(): after = lax.ppermute(leading, axis, down)]
  transfers between devices with their start and end apart: 16 -> 16, of which waited for: 12 -> 10; matrix products, arithmetic and copies ran while one was open for 2% -> 6% of each run, Pallas kernels for 0% -> 0%
where the time goes in v1:
time: 329 us
  Pallas kernels  206 us (63%)
  waiting for transfers between devices  40.5 us (12%)
  starting transfers between devices  35.9 us (11%)
  local copies, waits for them, and re-layouts  27.3 us (8%)
  other arithmetic  18.6 us (6%)
    pallas_call x2, Pallas kernels, feed(): pl.pallas_call(functools.partial(feed_kernel, last), out_shape=out_shape,...  152 us
    pallas_call x2, Pallas kernels, attention(): pl.pallas_call(attention_kernel, out_shape=(jax.ShapeDtypeStruct(shape, F...  53.8 us
    ppermute x8, waiting for transfers between devices, with_halo(): before = lax.ppermute(last, axis, up)  23.9 us
    ppermute x8, starting transfers between devices, with_halo(): after = lax.ppermute(leading, axis, down)  18.6 us
    ppermute x8, starting transfers between devices, with_halo(): before = lax.ppermute(last, axis, up)  17.3 us
    ppermute x8, waiting for transfers between devices, with_halo(): after = lax.ppermute(leading, axis, down)  16.6 us
    concatenate x4, other arithmetic, with_halo(): shard = jnp.concatenate(parts, axis=dim)  11 us
  transfers between devices with their start and end apart: 16, of which 10 were waited for; matrix products, arithmetic and copies ran while one was open for 6% of the time, Pallas kernels for 0%

profile of v1, /device:TPU:0, one launch (start us, length us, event | category | flops | bytes accessed | tf_op | source)
XLA Modules:
  0.0 328.9 jit_solution(2223294571068956112)
XLA Ops:
  0.0 1.6 convert_reduce_fusion
  1.6 1.8 multiply_reduce_fusion
  4.5 0.9 fusion.10
  5.4 4.9 %collective-permute-start = (bf16[6,48,512]{2,1,0:T(8,128)(2,1)}, bf16[6,48,512]{2,1,0:T(8,128)(2,1)S(1)}, u32[]{:S(2)}, u32[]{:S(2)}) collective-permute-start(bf16[6,48,512]{2,1,0:T(8,128)(2,1)} %get-tuple-element.37), channel_id=1, source_target_pairs={{0,1},{1,2},{2,3},{4,5},{5,6},{6,7},{8,9},{9,10},{10,11},{12,13},{... | collective-permute-start | bytes 884744 | tf_op jit(solution)/shard_map/ppermute | solution.py:35
  10.3 1.3 collective-permute-start.1
  11.7 1.8 slice_bitcast_fusion.4
  13.9 2.2 and.55
  16.4 4.5 %slice_bitcast_fusion = (bf16[2048,512]{1,0:T(8,128)(2,1)}, bf16[2048,512]{1,0:T(8,128)(2,1)}) fusion(bf16[2,2048,512]{2,1,0:T(8,128)(2,1)} %param.17), kind=kLoop, calls=%fused_computation.4 | loop fusion | bytes 8388608 | tf_op jit(solution)/shard_map/squeeze | solution.py:319
  20.9 1.0 and_select_fusion.bias_ref
  21.9 1.8 convert_element_type.6.stream_ref
  23.8 1.1 slice_bitcast_fusion.6
  25.1 0.9 pad_maximum_fusion.2
  26.1 3.5 %collective-permute-start.3 = (bf16[36,6,512]{2,1,0:T(8,128)(2,1)S(1)}, bf16[36,6,512]{2,1,0:T(8,128)(2,1)S(1)}, u32[]{:S(2)}, u32[]{:S(2)}) collective-permute-start(bf16[36,6,512]{2,1,0:T(8,128)(2,1)S(1)} %get-tuple-element.26), channel_id=1, source_target_pairs={{4,0},{8,4},{12,8},{16,12},{20,16},{24,20},{28,24},{0,28},{5,1},{9... | collective-permute-start | bytes 663560 | tf_op jit(solution)/shard_map/ppermute | solution.py:36
  29.6 0.6 fusion.12
  30.2 4.9 %collective-permute-done.2 = bf16[36,6,512]{2,1,0:T(8,128)(2,1)S(1)} collective-permute-done((bf16[36,6,512]{2,1,0:T(8,128)(2,1)S(1)}, bf16[36,6,512]{2,1,0:T(8,128)(2,1)S(1)}, u32[]{:S(2)}, u32[]{:S(2)}) %collective-permute-start.2) | collective-permute-done | bytes 221216 | tf_op jit(solution)/shard_map/ppermute | solution.py:35
  35.1 3.5 %maximum_maximum_fusion.ext_ref = bf16[36,64,512]{2,1,0:T(8,128)(2,1)} fusion(bf16[36,6,512]{2,1,0:T(8,128)(2,1)S(1)} %collective-permute-done.3, bf16[6,48,512]{2,1,0:T(8,128)(2,1)} %collective-permute-done.1, bf16[24,48,512]{2,1,0:T(8,128)(2,1)S(1)} %multiply_convert_fusion.own_ref, bf16[6,48,512]{2,1,0:T(8,128)(2,1)S(1)} %collective-permute-done, ...), kind=kLoop, calls=%fused_computation | loop fusion | flops 14155776 | bytes 4571264 | tf_op jit(solution)/shard_map/concatenate | solution.py:41
  38.6 26.9 %attend.2 = (f32[24,48,512]{2,1,0:T(8,128)}, bf16[24,48,512]{2,1,0:T(8,128)(2,1)}) custom-call(bf16[24,48,512]{2,1,0:T(8,128)(2,1)} %copy-done, bf16[36,64,512]{2,1,0:T(8,128)(2,1)} %maximum_maximum_fusion.ext_ref, bf16[512,1536]{1,0:T(8,128)(2,1)} %get-tuple-element.22.win_ref, bf16[512,512]{1,0:T(8,128)(2,1)} %get-tuple-element.40.wout_ref, ...), custom_call_target="tpu_custom_call" | custom-call | tf_op jit(solution)/shard_map/attend/pallas_call | solution.py:225
  65.4 1.0 fusion.9
  66.5 4.5 %collective-permute-start.4 = (bf16[3,48,512]{2,1,0:T(8,128)(2,1)S(1)}, bf16[3,48,512]{2,1,0:T(8,128)(2,1)S(1)}, u32[]{:S(2)}, u32[]{:S(2)}) collective-permute-start(bf16[3,48,512]{2,1,0:T(8,128)(2,1)S(1)} %get-tuple-element.36), channel_id=1, source_target_pairs={{0,1},{1,2},{2,3},{4,5},{5,6},{6,7},{8,9},{9,10},{10,11},{12,13},{... | collective-permute-start | bytes 442376 | tf_op jit(solution)/shard_map/ppermute | solution.py:35
  70.9 4.7 %slice_bitcast_fusion.1 = (bf16[512,2048]{1,0:T(8,128)(2,1)}, bf16[512,2048]{1,0:T(8,128)(2,1)}) fusion(bf16[2,512,2048]{2,1,0:T(8,128)(2,1)} %param.15), kind=kLoop, calls=%fused_computation.5 | loop fusion | bytes 8388608 | tf_op jit(solution)/shard_map/squeeze | solution.py:317
  75.7 1.4 collective-permute-start.5
  77.2 6.6 %collective-permute-done.5 = bf16[3,48,512]{2,1,0:T(8,128)(2,1)S(1)} collective-permute-done((bf16[3,48,512]{2,1,0:T(8,128)(2,1)S(1)}, bf16[3,48,512]{2,1,0:T(8,128)(2,1)S(1)}, u32[]{:S(2)}, u32[]{:S(2)}) %collective-permute-start.5) | collective-permute-done | bytes 147488 | tf_op jit(solution)/shard_map/ppermute | solution.py:36
  83.9 0.8 collective-permute-start.6
  84.7 2.8 collective-permute-start.7
  88.3 1.8 collective-permute-done.6
  90.1 2.4 maximum_maximum_fusion.2.ext_ref
  92.5 2.1 broadcast_in_dim.29.taps_ref
  94.6 77.2 %feed.2 = (f32[24,48,512]{2,1,0:T(8,128)}, bf16[24,48,512]{2,1,0:T(8,128)(2,1)}) custom-call(bf16[30,64,512]{2,1,0:T(8,128)(2,1)} %maximum_maximum_fusion.2.ext_ref, bf16[512,2048]{1,0:T(8,128)(2,1)} %get-tuple-element.20.expand_ref, bf16[7,7,16,2048]{3,2,1,0:T(8,128)(2,1)} %broadcast_in_dim.29.taps_ref, bf16[2048,512]{1,0:T(8,128)(2,1)} %get-tuple-element.18.shrink_ref, ...), custom_call_target="tpu_custom_call" | custom-call | tf_op jit(solution)/shard_map/feed/pallas_call | solution.py:249
  171.8 1.2 fusion.8
  173.0 5.2 %collective-permute-start.8 = (bf16[6,48,512]{2,1,0:T(8,128)(2,1)S(1)}, bf16[6,48,512]{2,1,0:T(8,128)(2,1)S(1)}, u32[]{:S(2)}, u32[]{:S(2)}) collective-permute-start(bf16[6,48,512]{2,1,0:T(8,128)(2,1)S(1)} %get-tuple-element.34), channel_id=1, source_target_pairs={{0,1},{1,2},{2,3},{4,5},{5,6},{6,7},{8,9},{9,10},{10,11},{12,13},{... | collective-permute-start | bytes 884744 | tf_op jit(solution)/shard_map/ppermute | solution.py:35
  178.2 1.3 collective-permute-start.9
  179.5 6.0 %collective-permute-done.8 = bf16[6,48,512]{2,1,0:T(8,128)(2,1)S(1)} collective-permute-done((bf16[6,48,512]{2,1,0:T(8,128)(2,1)S(1)}, bf16[6,48,512]{2,1,0:T(8,128)(2,1)S(1)}, u32[]{:S(2)}, u32[]{:S(2)}) %collective-permute-start.8) | collective-permute-done | bytes 294944 | tf_op jit(solution)/shard_map/ppermute | solution.py:35
  185.6 7.0 %collective-permute-done.9 = bf16[6,48,512]{2,1,0:T(8,128)(2,1)S(1)} collective-permute-done((bf16[6,48,512]{2,1,0:T(8,128)(2,1)S(1)}, bf16[6,48,512]{2,1,0:T(8,128)(2,1)S(1)}, u32[]{:S(2)}, u32[]{:S(2)}) %collective-permute-start.9) | collective-permute-done | bytes 294944 | tf_op jit(solution)/shard_map/ppermute | solution.py:36
  192.9 3.4 %collective-permute-start.11 = (bf16[36,6,512]{2,1,0:T(8,128)(2,1)S(1)}, bf16[36,6,512]{2,1,0:T(8,128)(2,1)S(1)}, u32[]{:S(2)}, u32[]{:S(2)}) collective-permute-start(bf16[36,6,512]{2,1,0:T(8,128)(2,1)S(1)} %get-tuple-element.24), channel_id=1, source_target_pairs={{4,0},{8,4},{12,8},{16,12},{20,16},{24,20},{28,24},{0,28},{5,1},{9... | collective-permute-start | bytes 663560 | tf_op jit(solution)/shard_map/ppermute | solution.py:36
  196.4 6.6 %collective-permute-done.10 = bf16[36,6,512]{2,1,0:T(8,128)(2,1)S(1)} collective-permute-done((bf16[36,6,512]{2,1,0:T(8,128)(2,1)S(1)}, bf16[36,6,512]{2,1,0:T(8,128)(2,1)S(1)}, u32[]{:S(2)}, u32[]{:S(2)}) %collective-permute-start.10) | collective-permute-done | bytes 221216 | tf_op jit(solution)/shard_map/ppermute | solution.py:35
  203.0 2.7 maximum_maximum_fusion.1.ext_ref
  205.7 26.9 %attend.3 = (f32[24,48,512]{2,1,0:T(8,128)}, bf16[24,48,512]{2,1,0:T(8,128)(2,1)}) custom-call(bf16[24,48,512]{2,1,0:T(8,128)(2,1)} %get-tuple-element.13.own_ref, bf16[36,64,512]{2,1,0:T(8,128)(2,1)} %maximum_maximum_fusion.1.ext_ref, bf16[512,1536]{1,0:T(8,128)(2,1)} %get-tuple-element.21.win_ref, bf16[512,512]{1,0:T(8,128)(2,1)} %get-tuple-element.39.wout_ref, ...), custom_call_target="tpu_custom_call" | custom-call | tf_op jit(solution)/shard_map/attend/pallas_call | solution.py:225
  232.6 1.0 fusion.7
  233.6 1.7 collective-permute-start.12
  235.3 1.3 collective-permute-start.13
  236.6 2.1 collective-permute-done.12
  238.7 1.3 constant_dynamic-update-slice_fusion.7
  240.1 2.8 collective-permute-done.13
  243.0 3.5 %collective-permute-start.15 = (bf16[30,3,512]{2,1,0:T(4,128)(2,1)S(1)}, bf16[30,3,512]{2,1,0:T(4,128)(2,1)S(1)}, u32[]{:S(2)}, u32[]{:S(2)}) collective-permute-start(bf16[30,3,512]{2,1,0:T(4,128)(2,1)S(1)} %get-tuple-element.28), channel_id=1, source_target_pairs={{4,0},{8,4},{12,8},{16,12},{20,16},{24,20},{28,24},{0,28},{5,1},{9... | collective-permute-start | bytes 276488 | tf_op jit(solution)/shard_map/ppermute | solution.py:36
  246.7 2.5 collective-permute-done.14
  249.2 2.4 maximum_maximum_fusion.3.ext_ref
  251.6 2.1 broadcast_in_dim.31.taps_ref
  253.7 75.2 %feed.3 = bf16[24,48,512]{2,1,0:T(8,128)(2,1)} custom-call(bf16[30,64,512]{2,1,0:T(8,128)(2,1)} %maximum_maximum_fusion.3.ext_ref, bf16[512,2048]{1,0:T(8,128)(2,1)} %get-tuple-element.19.expand_ref, bf16[7,7,16,2048]{3,2,1,0:T(8,128)(2,1)} %broadcast_in_dim.31.taps_ref, bf16[2048,512]{1,0:T(8,128)(2,1)} %get-tuple-element.17.shrink_ref, ...), custom_call_target="tpu_custom_call" | custom-call | tf_op jit(solution)/shard_map/feed/pallas_call | solution.py:249
  (64 shorter events, 3.8 us)
Async XLA Ops:
  0.0 4.0 %copy-start.1 = (bf16[24,48,512]{2,1,0:T(8,128)(2,1)S(1)}, bf16[24,48,512]{2,1,0:T(8,128)(2,1)}, u32[]{:S(2)}) copy-start(bf16[24,48,512]{2,1,0:T(8,128)(2,1)} %param.12) | copy-start | bytes 3538948
  0.0 3.4 %copy-start.8 = (f32[2,512]{1,0:T(2,128)S(1)}, f32[2,512]{1,0:T(2,128)}, u32[]{:S(2)}) copy-start(f32[2,512]{1,0:T(2,128)} %param.18) | copy-start | bytes 12292
  3.4 8.2 %copy-start.3 = (bf16[2,512,1536]{2,1,0:T(8,128)(2,1)S(1)}, bf16[2,512,1536]{2,1,0:T(8,128)(2,1)}, u32[]{:S(2)}) copy-start(bf16[2,512,1536]{2,1,0:T(8,128)(2,1)} %param.13) | copy-start | bytes 9437188
  4.5 30.6 %copy-start = (bf16[24,48,512]{2,1,0:T(8,128)(2,1)}, bf16[24,48,512]{2,1,0:T(8,128)(2,1)S(1)}, u32[]{:S(2)}) copy-start(bf16[24,48,512]{2,1,0:T(8,128)(2,1)S(1)} %multiply_convert_fusion.own_ref) | copy-start | bytes 3538948
  5.4 19.5 %collective-permute-start = (bf16[6,48,512]{2,1,0:T(8,128)(2,1)}, bf16[6,48,512]{2,1,0:T(8,128)(2,1)S(1)}, u32[]{:S(2)}, u32[]{:S(2)}) collective-permute-start(bf16[6,48,512]{2,1,0:T(8,128)(2,1)} %get-tuple-element.37), channel_id=1, source_target_pairs={{0,1},{1,2},{2,3},{4,5},{5,6},{6,7},{8,9},{9,10},{10,11},{12,13},{... | collective-permute-start | bytes 884744 | tf_op jit(solution)/shard_map/ppermute | solution.py:35
  10.3 14.8 %collective-permute-start.1 = (bf16[6,48,512]{2,1,0:T(8,128)(2,1)}, bf16[6,48,512]{2,1,0:T(8,128)(2,1)}, u32[]{:S(2)}, u32[]{:S(2)}) collective-permute-start(bf16[6,48,512]{2,1,0:T(8,128)(2,1)} %get-tuple-element.38), channel_id=1, source_target_pairs={{1,0},{2,1},{3,2},{5,4},{6,5},{7,6},{9,8},{10,9},{11,10},{13,12},{... | collective-permute-start | bytes 884744 | tf_op jit(solution)/shard_map/ppermute | solution.py:36
  11.6 1.9 copy-start.12
  11.6 2.0 copy-start.11
  11.6 4.5 %copy-start.10 = (pred[16,32]{1,0:T(8,128)(4,1)S(1)}, pred[16,32]{1,0:T(8,128)(4,1)}, u32[]{:S(2)}) copy-start(pred[16,32]{1,0:T(8,128)(4,1)} %constant.40) | copy-start | bytes 1540
  16.4 4.5 %copy-start.7 = (pred[6,64,512]{2,1,0:T(8,128)(4,1)S(1)}, pred[6,64,512]{2,1,0:T(8,128)(4,1)}, u32[]{:S(2)}) copy-start(pred[6,64,512]{2,1,0:T(8,128)(4,1)} %and.55) | copy-start | bytes 589828
  20.9 2.8 copy-start.6
  23.8 5.8 %copy-start.9 = (f32[2,512]{1,0:T(2,128)S(1)}, f32[2,512]{1,0:T(2,128)}, u32[]{:S(2)}) copy-start(f32[2,512]{1,0:T(2,128)} %param.19) | copy-start | bytes 12292
  26.0 9.1 %collective-permute-start.2 = (bf16[36,6,512]{2,1,0:T(8,128)(2,1)S(1)}, bf16[36,6,512]{2,1,0:T(8,128)(2,1)S(1)}, u32[]{:S(2)}, u32[]{:S(2)}) collective-permute-start(bf16[36,6,512]{2,1,0:T(8,128)(2,1)S(1)} %get-tuple-element.25), channel_id=1, source_target_pairs={{0,4},{4,8},{8,12},{12,16},{16,20},{20,24},{24,28},{28,0},{1,5},{5... | collective-permute-start | bytes 663560 | tf_op jit(solution)/shard_map/ppermute | solution.py:35
  26.1 9.0 %collective-permute-start.3 = (bf16[36,6,512]{2,1,0:T(8,128)(2,1)S(1)}, bf16[36,6,512]{2,1,0:T(8,128)(2,1)S(1)}, u32[]{:S(2)}, u32[]{:S(2)}) collective-permute-start(bf16[36,6,512]{2,1,0:T(8,128)(2,1)S(1)} %get-tuple-element.26), channel_id=1, source_target_pairs={{4,0},{8,4},{12,8},{16,12},{20,16},{24,20},{28,24},{0,28},{5,1},{9... | collective-permute-start | bytes 663560 | tf_op jit(solution)/shard_map/ppermute | solution.py:36
  66.4 10.7 %copy-start.4 = (bf16[24,48,512]{2,1,0:T(8,128)(2,1)S(1)}, bf16[24,48,512]{2,1,0:T(8,128)(2,1)}, u32[]{:S(2)}) copy-start(bf16[24,48,512]{2,1,0:T(8,128)(2,1)} %get-tuple-element.11) | copy-start | bytes 3538948
  66.5 10.6 %collective-permute-start.4 = (bf16[3,48,512]{2,1,0:T(8,128)(2,1)S(1)}, bf16[3,48,512]{2,1,0:T(8,128)(2,1)S(1)}, u32[]{:S(2)}, u32[]{:S(2)}) collective-permute-start(bf16[3,48,512]{2,1,0:T(8,128)(2,1)S(1)} %get-tuple-element.36), channel_id=1, source_target_pairs={{0,1},{1,2},{2,3},{4,5},{5,6},{6,7},{8,9},{9,10},{10,11},{12,13},{... | collective-permute-start | bytes 442376 | tf_op jit(solution)/shard_map/ppermute | solution.py:35
  75.7 11.9 %copy-start.5 = (bf16[2,7,7,2048]{3,0,2,1:T(2,128)(2,1)S(1)}, bf16[2,7,7,2048]{3,0,2,1:T(2,128)(2,1)}, u32[]{:S(2)}) copy-start(bf16[2,7,7,2048]{3,0,2,1:T(2,128)(2,1)} %param.16) | copy-start | bytes 1204228
  75.7 8.1 %collective-permute-start.5 = (bf16[3,48,512]{2,1,0:T(8,128)(2,1)S(1)}, bf16[3,48,512]{2,1,0:T(8,128)(2,1)S(1)}, u32[]{:S(2)}, u32[]{:S(2)}) collective-permute-start(bf16[3,48,512]{2,1,0:T(8,128)(2,1)S(1)} %get-tuple-element.35), channel_id=1, source_target_pairs={{1,0},{2,1},{3,2},{5,4},{6,5},{7,6},{9,8},{10,9},{11,10},{13,12},{... | collective-permute-start | bytes 442376 | tf_op jit(solution)/shard_map/ppermute | solution.py:36
  83.9 6.2 %collective-permute-start.6 = (bf16[30,3,512]{2,1,0:T(4,128)(2,1)S(1)}, bf16[30,3,512]{2,1,0:T(4,128)(2,1)S(1)}, u32[]{:S(2)}, u32[]{:S(2)}) collective-permute-start(bf16[30,3,512]{2,1,0:T(4,128)(2,1)S(1)} %get-tuple-element.29), channel_id=1, source_target_pairs={{0,4},{4,8},{8,12},{12,16},{16,20},{20,24},{24,28},{28,0},{1,5},{5... | collective-permute-start | bytes 276488 | tf_op jit(solution)/shard_map/ppermute | solution.py:35
  84.7 5.4 %collective-permute-start.7 = (bf16[30,3,512]{2,1,0:T(4,128)(2,1)S(1)}, bf16[30,3,512]{2,1,0:T(4,128)(2,1)S(1)}, u32[]{:S(2)}, u32[]{:S(2)}) collective-permute-start(bf16[30,3,512]{2,1,0:T(4,128)(2,1)S(1)} %get-tuple-element.30), channel_id=1, source_target_pairs={{4,0},{8,4},{12,8},{16,12},{20,16},{24,20},{28,24},{0,28},{5,1},{9... | collective-permute-start | bytes 276488 | tf_op jit(solution)/shard_map/ppermute | solution.py:36
  171.8 13.7 %copy-start.2 = (bf16[24,48,512]{2,1,0:T(8,128)(2,1)S(1)}, bf16[24,48,512]{2,1,0:T(8,128)(2,1)}, u32[]{:S(2)}) copy-start(bf16[24,48,512]{2,1,0:T(8,128)(2,1)} %get-tuple-element.13.own_ref) | copy-start | bytes 3538948
  173.0 12.5 %collective-permute-start.8 = (bf16[6,48,512]{2,1,0:T(8,128)(2,1)S(1)}, bf16[6,48,512]{2,1,0:T(8,128)(2,1)S(1)}, u32[]{:S(2)}, u32[]{:S(2)}) collective-permute-start(bf16[6,48,512]{2,1,0:T(8,128)(2,1)S(1)} %get-tuple-element.34), channel_id=1, source_target_pairs={{0,1},{1,2},{2,3},{4,5},{5,6},{6,7},{8,9},{9,10},{10,11},{12,13},{... | collective-permute-start | bytes 884744 | tf_op jit(solution)/shard_map/ppermute | solution.py:35
  178.2 14.5 %collective-permute-start.9 = (bf16[6,48,512]{2,1,0:T(8,128)(2,1)S(1)}, bf16[6,48,512]{2,1,0:T(8,128)(2,1)S(1)}, u32[]{:S(2)}, u32[]{:S(2)}) collective-permute-start(bf16[6,48,512]{2,1,0:T(8,128)(2,1)S(1)} %get-tuple-element.33), channel_id=1, source_target_pairs={{1,0},{2,1},{3,2},{5,4},{6,5},{7,6},{9,8},{10,9},{11,10},{13,12},{... | collective-permute-start | bytes 884744 | tf_op jit(solution)/shard_map/ppermute | solution.py:36
  192.8 10.2 %collective-permute-start.10 = (bf16[36,6,512]{2,1,0:T(8,128)(2,1)S(1)}, bf16[36,6,512]{2,1,0:T(8,128)(2,1)S(1)}, u32[]{:S(2)}, u32[]{:S(2)}) collective-permute-start(bf16[36,6,512]{2,1,0:T(8,128)(2,1)S(1)} %get-tuple-element.23), channel_id=1, source_target_pairs={{0,4},{4,8},{8,12},{12,16},{16,20},{20,24},{24,28},{28,0},{1,5},{5... | collective-permute-start | bytes 663560 | tf_op jit(solution)/shard_map/ppermute | solution.py:35
  192.9 10.0 %collective-permute-start.11 = (bf16[36,6,512]{2,1,0:T(8,128)(2,1)S(1)}, bf16[36,6,512]{2,1,0:T(8,128)(2,1)S(1)}, u32[]{:S(2)}, u32[]{:S(2)}) collective-permute-start(bf16[36,6,512]{2,1,0:T(8,128)(2,1)S(1)} %get-tuple-element.24), channel_id=1, source_target_pairs={{4,0},{8,4},{12,8},{16,12},{20,16},{24,20},{28,24},{0,28},{5,1},{9... | collective-permute-start | bytes 663560 | tf_op jit(solution)/shard_map/ppermute | solution.py:36
  233.6 5.1 %collective-permute-start.12 = (bf16[3,48,512]{2,1,0:T(8,128)(2,1)S(1)}, bf16[3,48,512]{2,1,0:T(8,128)(2,1)S(1)}, u32[]{:S(2)}, u32[]{:S(2)}) collective-permute-start(bf16[3,48,512]{2,1,0:T(8,128)(2,1)S(1)} %get-tuple-element.32), channel_id=1, source_target_pairs={{0,1},{1,2},{2,3},{4,5},{5,6},{6,7},{8,9},{9,10},{10,11},{12,13},{... | collective-permute-start | bytes 442376 | tf_op jit(solution)/shard_map/ppermute | solution.py:35
  235.3 7.5 %collective-permute-start.13 = (bf16[3,48,512]{2,1,0:T(8,128)(2,1)S(1)}, bf16[3,48,512]{2,1,0:T(8,128)(2,1)S(1)}, u32[]{:S(2)}, u32[]{:S(2)}) collective-permute-start(bf16[3,48,512]{2,1,0:T(8,128)(2,1)S(1)} %get-tuple-element.31), channel_id=1, source_target_pairs={{1,0},{2,1},{3,2},{5,4},{6,5},{7,6},{9,8},{10,9},{11,10},{13,12},{... | collective-permute-start | bytes 442376 | tf_op jit(solution)/shard_map/ppermute | solution.py:36
  243.0 6.3 %collective-permute-start.14 = (bf16[30,3,512]{2,1,0:T(4,128)(2,1)S(1)}, bf16[30,3,512]{2,1,0:T(4,128)(2,1)S(1)}, u32[]{:S(2)}, u32[]{:S(2)}) collective-permute-start(bf16[30,3,512]{2,1,0:T(4,128)(2,1)S(1)} %get-tuple-element.27), channel_id=1, source_target_pairs={{0,4},{4,8},{8,12},{12,16},{16,20},{20,24},{24,28},{28,0},{1,5},{5... | collective-permute-start | bytes 276488 | tf_op jit(solution)/shard_map/ppermute | solution.py:35
  243.0 6.2 %collective-permute-start.15 = (bf16[30,3,512]{2,1,0:T(4,128)(2,1)S(1)}, bf16[30,3,512]{2,1,0:T(4,128)(2,1)S(1)}, u32[]{:S(2)}, u32[]{:S(2)}) collective-permute-start(bf16[30,3,512]{2,1,0:T(4,128)(2,1)S(1)} %get-tuple-element.28), channel_id=1, source_target_pairs={{4,0},{8,4},{12,8},{16,12},{20,16},{24,20},{28,24},{0,28},{5,1},{9... | collective-permute-start | bytes 276488 | tf_op jit(solution)/shard_map/ppermute | solution.py:36

commit v2 on v1

--- a/solution.py
+++ b/solution.py
@@ -19,6 +19,7 @@
 K_LAT = Q_LAT + 2 * RADIUS
 K_LON = 32
 GROUP = 4
+LANES = 256
 NEG = -1e30
 VMEM_LIMIT = 60 * 1024 * 1024
 F32 = jnp.float32
@@ -148,7 +149,7 @@
     def _(r):
         x = mixed_ref[pl.ds(r * 4, 4)].reshape(4 * width, channels)
         y = jnp.dot(x, wout_ref[...], preferred_element_type=F32)
-        y = y + stream_ref[pl.ds(r * 4, 4)].reshape(4 * width, channels)
+        y = y + stream_ref[pl.ds(r * 4, 4)].reshape(4 * width, channels).astype(F32)
         out_ref[pl.ds(r * 4, 4)] = y.reshape(4, width, channels)
         normed_ref[pl.ds(r * 4, 4)] = norm_rows(y, gain_ref[...]).reshape(4, width, channels)
 
@@ -162,6 +163,7 @@
     rows, wide, _ = ext_ref.shape
     chunk = expand_ref.shape[1]
     side = 2 * CONV_RADIUS + 1
+    reach = -(-(width + side - 1) // 8) * 8
     step = pl.program_id(0)
 
     @pl.loop(0, rows // 5)
@@ -170,18 +172,18 @@
         y = jnp.dot(x, expand_ref[...], preferred_element_type=F32)
         hid_ref[pl.ds(r * 5, 5)] = y.astype(BF16).reshape(5, wide, chunk)
 
-    parts = chunk // 128
+    parts = chunk // LANES
 
     def conv_row(n, carry):
         i = n // parts
-        lanes = pl.ds(pl.multiple_of((n % parts) * 128, 128), 128)
-        lines = [hid_ref[i + a, :, lanes].reshape(wide // 16, 16, 128) for a in range(side)]
+        lanes = pl.ds(pl.multiple_of((n % parts) * LANES, LANES), LANES)
+        lines = [hid_ref[i + a, 0:reach, lanes].reshape(reach // 8, 8, LANES) for a in range(side)]
         total = None
         for b in range(side):
             p = lines[0] * taps_ref[0, b, :, lanes]
             for a in range(1, side):
                 p = p + lines[a] * taps_ref[a, b, :, lanes]
-            p = p.reshape(wide, 128).astype(F32)[b : b + width]
+            p = p.reshape(reach, LANES).astype(F32)[b : b + width]
             total = p if total is None else total + p
         act_ref[i, :, lanes] = gelu(total).astype(BF16)
         return carry
@@ -214,19 +216,25 @@
                 normed_ref[rs] = z.reshape(4, width, channels)
 
 
+def pick(shape, layer):
+    rest = shape[1:]
+    return pl.BlockSpec((None,) + rest, lambda *_: (layer,) + (0,) * len(rest))
+
+
 def full(shape):
     return pl.BlockSpec(shape, lambda *_: (0,) * len(shape))
 
 
-def attention(own, ext, w_in, w_out, bias, stream, gain):
+def attention(layer, own, ext, w_in, w_out, bias, stream, gain):
     shape = own.shape
     height, width, channels = shape
     args = (own, ext, w_in, w_out, bias, stream, gain)
     return pl.pallas_call(
         attention_kernel,
         out_shape=(jax.ShapeDtypeStruct(shape, F32), jax.ShapeDtypeStruct(shape, BF16)),
-        in_specs=[pl.BlockSpec(memory_space=pltpu.VMEM)] * len(args),
-        out_specs=(pl.BlockSpec(memory_space=pltpu.VMEM),) * 2,
+        grid=(1,),
+        in_specs=[pick(a.shape, layer) if a is w_in or a is w_out else full(a.shape) for a in args],
+        out_specs=(full(shape),) * 2,
         scratch_shapes=[
             pltpu.VMEM(shape, BF16),
             pltpu.VMEM(ext.shape[:2] + (2 * channels,), BF16),
@@ -237,10 +245,10 @@
     )(*args)
 
 
-def feed(last, ext, expand, taps, shrink, stream, gain):
+def feed(last, layer, ext, expand, taps, shrink, stream, gain):
     shape = stream.shape
     height, width, channels = shape
-    units = expand.shape[1]
+    units = expand.shape[2]
     chunk = min(512, units)
     side = 2 * CONV_RADIUS + 1
     out_shape = [jax.ShapeDtypeStruct(shape, BF16 if last else F32)]
@@ -252,9 +260,9 @@
         grid=(units // chunk,),
         in_specs=[
             full(ext.shape),
-            pl.BlockSpec((channels, chunk), lambda j: (0, j)),
-            pl.BlockSpec((side, side, 16, chunk), lambda j: (0, 0, 0, j)),
-            pl.BlockSpec((chunk, channels), lambda j: (j, 0)),
+            pl.BlockSpec((None, channels, chunk), lambda j: (layer, 0, j)),
+            pl.BlockSpec((side, side, 8, chunk), lambda j: (0, 0, 0, j)),
+            pl.BlockSpec((None, chunk, channels), lambda j: (layer, j, 0)),
             full(shape),
             full(gain.shape),
         ],
@@ -296,27 +304,29 @@
     norm_feedforward,
 ):
     bias = score_bias(state.shape[0])
-    stream = state.astype(F32)
-    normed = norm_rows(stream, norm_attention[0])
+    stream = state
+    normed = norm_rows(state.astype(F32), norm_attention[0])
     for layer in range(LAYERS):
         last = layer == LAYERS - 1
         taps = depth_kernel[layer]
-        taps = jnp.broadcast_to(taps[:, :, None, :], taps.shape[:2] + (16, taps.shape[2]))
+        taps = jnp.broadcast_to(taps[:, :, None, :], taps.shape[:2] + (8, taps.shape[2]))
         stream, normed_ff = attention(
+            layer,
             normed,
             halo(normed, RADIUS),
-            attention_in[layer],
-            attention_out[layer],
+            attention_in,
+            attention_out,
             bias,
             stream,
             norm_feedforward[layer][None],
         )
         outs = feed(
             last,
+            layer,
             halo(normed_ff, CONV_RADIUS),
-            expand_weight[layer],
+            expand_weight,
             taps,
-            shrink_weight[layer],
+            shrink_weight,
             stream,
             norm_attention[min(layer + 1, LAYERS - 1)][None],
         )

time: 329 us -> 263 us (0.80)
  Pallas kernels: 206 us -> 154 us
  local copies, waits for them, and re-layouts: 27.3 us -> 13.7 us
  waiting for transfers between devices: 40.5 us -> 47.9 us
  other arithmetic: 18.6 us -> 14 us
  starting transfers between devices: 35.9 us -> 32.1 us
    pallas_call x2, Pallas kernels: 152 us -> 101 us  [feed(): pl.pallas_call(functools.partial(feed_kernel, last), out_shape=out_shape,...]
    squeeze x4 -> x0, local copies, waits for them, and re-layouts: 12.2 us -> none  [the longest x1 4.74 us: per_device(): expand_weight[layer]]
    ppermute x8, waiting for transfers between devices: 16.6 us -> 20.7 us  [with_halo(): after = lax.ppermute(leading, axis, down)]
    ppermute x8, starting transfers between devices: 17.3 us -> 13.5 us  [with_halo(): before = lax.ppermute(last, axis, up)]
  transfers between devices with their start and end apart: 16 -> 16, of which waited for: 10 -> 12; matrix products, arithmetic and copies ran while one was open for 6% -> 3% of each run, Pallas kernels for 0% -> 0%
where the time goes in v2:
time: 263 us; the launch traced here: 262 us
  Pallas kernels  154 us (59%)
  waiting for transfers between devices  47.9 us (18%)
  starting transfers between devices  32.1 us (12%)
  other arithmetic  14 us (5%)
  local copies, waits for them, and re-layouts  13.7 us (5%)
    pallas_call x2, Pallas kernels, feed(): pl.pallas_call(functools.partial(feed_kernel, last), out_shape=out_shape,...  101 us
    pallas_call x2, Pallas kernels, attention(): pl.pallas_call(attention_kernel, out_shape=(jax.ShapeDtypeStruct(shape, F...  53.5 us
    ppermute x8, waiting for transfers between devices, with_halo(): before = lax.ppermute(last, axis, up)  27.2 us
    ppermute x8, waiting for transfers between devices, with_halo(): after = lax.ppermute(leading, axis, down)  20.7 us
    ppermute x8, starting transfers between devices, with_halo(): after = lax.ppermute(leading, axis, down)  18.6 us
    ppermute x8, starting transfers between devices, with_halo(): before = lax.ppermute(last, axis, up)  13.5 us
    concatenate x4, other arithmetic, with_halo(): shard = jnp.concatenate(parts, axis=dim)  10.1 us
  transfers between devices with their start and end apart: 16, of which 12 were waited for; matrix products, arithmetic and copies ran while one was open for 3% of the time, Pallas kernels for 0%

profile of v2, /device:TPU:0, one launch (start us, length us, event | category | flops | bytes accessed | tf_op | source)
XLA Modules:
  0.0 262.4 jit_solution(12605715031363146223)
XLA Ops:
  0.0 1.6 convert_reduce_fusion
  1.6 0.6 fusion.2
  2.3 0.6 fusion.18
  2.9 0.4 fusion.4.own_ref
  3.4 4.9 %collective-permute-start = (bf16[6,48,512]{2,1,0:T(8,128)(2,1)S(1)}, bf16[6,48,512]{2,1,0:T(8,128)(2,1)S(1)}, u32[]{:S(2)}, u32[]{:S(2)}) collective-permute-start(bf16[6,48,512]{2,1,0:T(8,128)(2,1)S(1)} %get-tuple-element.31), channel_id=1, source_target_pairs={{0,1},{1,2},{2,3},{4,5},{5,6},{6,7},{8,9},{9,10},{10,11},{12,13},{... | collective-permute-start | bytes 884744 | tf_op jit(solution)/shard_map/ppermute | solution.py:36
  8.3 1.3 collective-permute-start.1
  10.0 1.6 and.55
  12.0 1.1 and_select_fusion.bias_ref
  13.1 1.4 collective-permute-done
  14.5 8.3 %collective-permute-done.1 = bf16[6,48,512]{2,1,0:T(8,128)(2,1)S(1)} collective-permute-done((bf16[6,48,512]{2,1,0:T(8,128)(2,1)S(1)}, bf16[6,48,512]{2,1,0:T(8,128)(2,1)S(1)}, u32[]{:S(2)}, u32[]{:S(2)}) %collective-permute-start.1) | collective-permute-done | bytes 294944 | tf_op jit(solution)/shard_map/ppermute | solution.py:37
  22.9 3.5 %collective-permute-start.3 = (bf16[36,6,512]{2,1,0:T(8,128)(2,1)S(1)}, bf16[36,6,512]{2,1,0:T(8,128)(2,1)S(1)}, u32[]{:S(2)}, u32[]{:S(2)}) collective-permute-start(bf16[36,6,512]{2,1,0:T(8,128)(2,1)S(1)} %get-tuple-element.20), channel_id=1, source_target_pairs={{4,0},{8,4},{12,8},{16,12},{20,16},{24,20},{28,24},{0,28},{5,1},{9... | collective-permute-start | bytes 663560 | tf_op jit(solution)/shard_map/ppermute | solution.py:37
  26.5 0.6 fusion.17
  27.1 4.9 %collective-permute-done.2 = bf16[36,6,512]{2,1,0:T(8,128)(2,1)S(1)} collective-permute-done((bf16[36,6,512]{2,1,0:T(8,128)(2,1)S(1)}, bf16[36,6,512]{2,1,0:T(8,128)(2,1)S(1)}, u32[]{:S(2)}, u32[]{:S(2)}) %collective-permute-start.2) | collective-permute-done | bytes 221216 | tf_op jit(solution)/shard_map/ppermute | solution.py:36
  31.9 2.5 maximum_maximum_fusion.ext_ref
  34.4 26.6 %attend.2 = (f32[24,48,512]{2,1,0:T(8,128)}, bf16[24,48,512]{2,1,0:T(8,128)(2,1)}) custom-call(bf16[24,48,512]{2,1,0:T(8,128)(2,1)} %copy-done, bf16[36,64,512]{2,1,0:T(8,128)(2,1)} %maximum_maximum_fusion.ext_ref, bf16[2,512,1536]{2,1,0:T(8,128)(2,1)} %win_ref.3, bf16[2,512,512]{2,1,0:T(8,128)(2,1)} %wout_ref.3, f32[6,64,512]{2,1,0:T(8,128)} %and_select_fusion.bias_ref, ...), custom_call_target="tpu_custom_call" | custom-call | tf_op jit(solution)/shard_map/attend/pallas_call | solution.py:232
  61.0 1.1 fusion.14
  62.1 3.4 %collective-permute-start.4 = (bf16[3,48,512]{2,1,0:T(8,128)(2,1)S(1)}, bf16[3,48,512]{2,1,0:T(8,128)(2,1)S(1)}, u32[]{:S(2)}, u32[]{:S(2)}) collective-permute-start(bf16[3,48,512]{2,1,0:T(8,128)(2,1)S(1)} %get-tuple-element.30), channel_id=1, source_target_pairs={{0,1},{1,2},{2,3},{4,5},{5,6},{6,7},{8,9},{9,10},{10,11},{12,13},{... | collective-permute-start | bytes 442376 | tf_op jit(solution)/shard_map/ppermute | solution.py:36
  65.5 1.3 collective-permute-start.5
  66.8 2.0 collective-permute-done.4
  68.8 1.3 constant_dynamic-update-slice_fusion.1
  70.1 3.3 %collective-permute-done.5 = bf16[3,48,512]{2,1,0:T(8,128)(2,1)S(1)} collective-permute-done((bf16[3,48,512]{2,1,0:T(8,128)(2,1)S(1)}, bf16[3,48,512]{2,1,0:T(8,128)(2,1)S(1)}, u32[]{:S(2)}, u32[]{:S(2)}) %collective-permute-start.5) | collective-permute-done | bytes 147488 | tf_op jit(solution)/shard_map/ppermute | solution.py:37
  73.6 0.5 collective-permute-start.6
  74.1 3.1 %collective-permute-start.7 = (bf16[30,3,512]{2,1,0:T(4,128)(2,1)S(1)}, bf16[30,3,512]{2,1,0:T(4,128)(2,1)S(1)}, u32[]{:S(2)}, u32[]{:S(2)}) collective-permute-start(bf16[30,3,512]{2,1,0:T(4,128)(2,1)S(1)} %get-tuple-element.24), channel_id=1, source_target_pairs={{4,0},{8,4},{12,8},{16,12},{20,16},{24,20},{28,24},{0,28},{5,1},{9... | collective-permute-start | bytes 276488 | tf_op jit(solution)/shard_map/ppermute | solution.py:37
  77.2 0.6 fusion.16
  78.0 1.9 collective-permute-done.6
  79.8 2.4 maximum_maximum_fusion.2.ext_ref
  82.3 1.5 broadcast_in_dim.29.taps_ref
  83.7 51.4 %feed.2 = (f32[24,48,512]{2,1,0:T(8,128)}, bf16[24,48,512]{2,1,0:T(8,128)(2,1)}) custom-call(bf16[30,64,512]{2,1,0:T(8,128)(2,1)} %maximum_maximum_fusion.2.ext_ref, bf16[2,512,2048]{2,1,0:T(8,128)(2,1)} %expand_ref.3, bf16[7,7,8,2048]{3,2,1,0:T(8,128)(2,1)} %broadcast_in_dim.29.taps_ref, bf16[2,2048,512]{2,1,0:T(8,128)(2,1)} %shrink_ref.3, ...), custom_call_target="tpu_custom_call" | custom-call | tf_op jit(solution)/shard_map/feed/pallas_call | solution.py:257
  135.1 1.2 fusion.13
  136.3 2.5 collective-permute-start.8
  138.8 1.3 collective-permute-start.9
  140.1 5.9 %collective-permute-done.8 = bf16[6,48,512]{2,1,0:T(8,128)(2,1)S(1)} collective-permute-done((bf16[6,48,512]{2,1,0:T(8,128)(2,1)S(1)}, bf16[6,48,512]{2,1,0:T(8,128)(2,1)S(1)}, u32[]{:S(2)}, u32[]{:S(2)}) %collective-permute-start.8) | collective-permute-done | bytes 294944 | tf_op jit(solution)/shard_map/ppermute | solution.py:36
  146.2 6.4 %collective-permute-done.9 = bf16[6,48,512]{2,1,0:T(8,128)(2,1)S(1)} collective-permute-done((bf16[6,48,512]{2,1,0:T(8,128)(2,1)S(1)}, bf16[6,48,512]{2,1,0:T(8,128)(2,1)S(1)}, u32[]{:S(2)}, u32[]{:S(2)}) %collective-permute-start.9) | collective-permute-done | bytes 294944 | tf_op jit(solution)/shard_map/ppermute | solution.py:37
  152.9 3.3 %collective-permute-start.11 = (bf16[36,6,512]{2,1,0:T(8,128)(2,1)S(1)}, bf16[36,6,512]{2,1,0:T(8,128)(2,1)S(1)}, u32[]{:S(2)}, u32[]{:S(2)}) collective-permute-start(bf16[36,6,512]{2,1,0:T(8,128)(2,1)S(1)} %get-tuple-element.18), channel_id=1, source_target_pairs={{4,0},{8,4},{12,8},{16,12},{20,16},{24,20},{28,24},{0,28},{5,1},{9... | collective-permute-start | bytes 663560 | tf_op jit(solution)/shard_map/ppermute | solution.py:37
  156.3 6.9 %collective-permute-done.10 = bf16[36,6,512]{2,1,0:T(8,128)(2,1)S(1)} collective-permute-done((bf16[36,6,512]{2,1,0:T(8,128)(2,1)S(1)}, bf16[36,6,512]{2,1,0:T(8,128)(2,1)S(1)}, u32[]{:S(2)}, u32[]{:S(2)}) %collective-permute-start.10) | collective-permute-done | bytes 221216 | tf_op jit(solution)/shard_map/ppermute | solution.py:36
  163.1 2.8 %maximum_maximum_fusion.1.ext_ref = bf16[36,64,512]{2,1,0:T(8,128)(2,1)} fusion(bf16[36,6,512]{2,1,0:T(8,128)(2,1)S(1)} %collective-permute-done.11, bf16[36,48,512]{2,1,0:T(8,128)(2,1)S(1)} %constant_dynamic-update-slice_fusion.3, bf16[36,6,512]{2,1,0:T(8,128)(2,1)S(1)} %collective-permute-done.10, bf16[64]{0:T(256)(128)(2,1)S(1)} %pad.17.clone), kind=kLoop, calls=%fused_computation.8 | loop fusion | flops 9437184 | bytes 4571264 | tf_op jit(solution)/shard_map/concatenate | solution.py:42
  165.9 26.9 %attend.3 = (f32[24,48,512]{2,1,0:T(8,128)}, bf16[24,48,512]{2,1,0:T(8,128)(2,1)}) custom-call(bf16[24,48,512]{2,1,0:T(8,128)(2,1)} %get-tuple-element.13.own_ref, bf16[36,64,512]{2,1,0:T(8,128)(2,1)} %maximum_maximum_fusion.1.ext_ref, bf16[2,512,1536]{2,1,0:T(8,128)(2,1)} %win_ref.3, bf16[2,512,512]{2,1,0:T(8,128)(2,1)} %wout_ref.3, ...), custom_call_target="tpu_custom_call" | custom-call | tf_op jit(solution)/shard_map/attend/pallas_call | solution.py:232
  192.8 1.0 fusion.12
  193.8 1.8 collective-permute-start.12
  195.6 1.3 collective-permute-start.13
  196.9 1.8 collective-permute-done.12
  198.8 1.3 constant_dynamic-update-slice_fusion.7
  200.1 2.8 %collective-permute-done.13 = bf16[3,48,512]{2,1,0:T(8,128)(2,1)S(1)} collective-permute-done((bf16[3,48,512]{2,1,0:T(8,128)(2,1)S(1)}, bf16[3,48,512]{2,1,0:T(8,128)(2,1)S(1)}, u32[]{:S(2)}, u32[]{:S(2)}) %collective-permute-start.13) | collective-permute-done | bytes 147488 | tf_op jit(solution)/shard_map/ppermute | solution.py:37
  203.1 3.5 %collective-permute-start.15 = (bf16[30,3,512]{2,1,0:T(4,128)(2,1)S(1)}, bf16[30,3,512]{2,1,0:T(4,128)(2,1)S(1)}, u32[]{:S(2)}, u32[]{:S(2)}) collective-permute-start(bf16[30,3,512]{2,1,0:T(4,128)(2,1)S(1)} %get-tuple-element.22), channel_id=1, source_target_pairs={{4,0},{8,4},{12,8},{16,12},{20,16},{24,20},{28,24},{0,28},{5,1},{9... | collective-permute-start | bytes 276488 | tf_op jit(solution)/shard_map/ppermute | solution.py:37
  206.7 2.4 collective-permute-done.14
  209.2 2.4 maximum_maximum_fusion.3.ext_ref
  211.6 1.5 broadcast_in_dim.31.taps_ref
  213.0 49.4 %feed.3 = bf16[24,48,512]{2,1,0:T(8,128)(2,1)} custom-call(bf16[30,64,512]{2,1,0:T(8,128)(2,1)} %maximum_maximum_fusion.3.ext_ref, bf16[2,512,2048]{2,1,0:T(8,128)(2,1)} %expand_ref.3, bf16[7,7,8,2048]{3,2,1,0:T(8,128)(2,1)} %broadcast_in_dim.31.taps_ref, bf16[2,2048,512]{2,1,0:T(8,128)(2,1)} %shrink_ref.3, f32[24,48,512]{2,1,0:T(8,128)} %get-tuple-element.16.stream_ref, ...), custom_call_target="tpu_custom_call" | custom-call | tf_op jit(solution)/shard_map/feed/pallas_call | solution.py:257
  (51 shorter events, 2.1 us)
Async XLA Ops:
  0.0 1.6 copy-start.1
  0.0 2.2 copy-start.4
  2.2 7.4 %copy-start.8 = (s32[6,1]{0,1:T(1,128)S(1)}, s32[6,1]{0,1:T(1,128)}, u32[]{:S(2)}) copy-start(s32[6,1]{0,1:T(1,128)} %constant.34.clone) | copy-start | bytes 76
  2.2 7.5 %copy-start.7 = (pred[4,16]{1,0:T(4,128)(4,1)S(1)}, pred[4,16]{1,0:T(4,128)(4,1)}, u32[]{:S(2)}) copy-start(pred[4,16]{1,0:T(4,128)(4,1)} %constant.38) | copy-start | bytes 196
  3.3 28.6 %copy-start = (bf16[24,48,512]{2,1,0:T(8,128)(2,1)}, bf16[24,48,512]{2,1,0:T(8,128)(2,1)S(1)}, u32[]{:S(2)}) copy-start(bf16[24,48,512]{2,1,0:T(8,128)(2,1)S(1)} %fusion.4.own_ref) | copy-start | bytes 3538948
  3.3 8.2 %copy-start.6 = (pred[16,32]{1,0:T(8,128)(4,1)S(1)}, pred[16,32]{1,0:T(8,128)(4,1)}, u32[]{:S(2)}) copy-start(pred[16,32]{1,0:T(8,128)(4,1)} %constant.40) | copy-start | bytes 1540
  3.4 11.1 %collective-permute-start = (bf16[6,48,512]{2,1,0:T(8,128)(2,1)S(1)}, bf16[6,48,512]{2,1,0:T(8,128)(2,1)S(1)}, u32[]{:S(2)}, u32[]{:S(2)}) collective-permute-start(bf16[6,48,512]{2,1,0:T(8,128)(2,1)S(1)} %get-tuple-element.31), channel_id=1, source_target_pairs={{0,1},{1,2},{2,3},{4,5},{5,6},{6,7},{8,9},{9,10},{10,11},{12,13},{... | collective-permute-start | bytes 884744 | tf_op jit(solution)/shard_map/ppermute | solution.py:36
  8.3 14.5 %collective-permute-start.1 = (bf16[6,48,512]{2,1,0:T(8,128)(2,1)S(1)}, bf16[6,48,512]{2,1,0:T(8,128)(2,1)S(1)}, u32[]{:S(2)}, u32[]{:S(2)}) collective-permute-start(bf16[6,48,512]{2,1,0:T(8,128)(2,1)S(1)} %get-tuple-element.32), channel_id=1, source_target_pairs={{1,0},{2,1},{3,2},{5,4},{6,5},{7,6},{9,8},{10,9},{11,10},{13,12},{... | collective-permute-start | bytes 884744 | tf_op jit(solution)/shard_map/ppermute | solution.py:37
  11.6 14.9 %copy-start.5 = (f32[2,512]{1,0:T(2,128)S(1)}, f32[2,512]{1,0:T(2,128)}, u32[]{:S(2)}) copy-start(f32[2,512]{1,0:T(2,128)} %param.19) | copy-start | bytes 12292
  22.9 9.1 %collective-permute-start.2 = (bf16[36,6,512]{2,1,0:T(8,128)(2,1)S(1)}, bf16[36,6,512]{2,1,0:T(8,128)(2,1)S(1)}, u32[]{:S(2)}, u32[]{:S(2)}) collective-permute-start(bf16[36,6,512]{2,1,0:T(8,128)(2,1)S(1)} %get-tuple-element.19), channel_id=1, source_target_pairs={{0,4},{4,8},{8,12},{12,16},{16,20},{20,24},{24,28},{28,0},{1,5},{5... | collective-permute-start | bytes 663560 | tf_op jit(solution)/shard_map/ppermute | solution.py:36
  22.9 9.0 %collective-permute-start.3 = (bf16[36,6,512]{2,1,0:T(8,128)(2,1)S(1)}, bf16[36,6,512]{2,1,0:T(8,128)(2,1)S(1)}, u32[]{:S(2)}, u32[]{:S(2)}) collective-permute-start(bf16[36,6,512]{2,1,0:T(8,128)(2,1)S(1)} %get-tuple-element.20), channel_id=1, source_target_pairs={{4,0},{8,4},{12,8},{16,12},{20,16},{24,20},{28,24},{0,28},{5,1},{9... | collective-permute-start | bytes 663560 | tf_op jit(solution)/shard_map/ppermute | solution.py:37
  61.0 16.1 %copy-start.3 = (bf16[2,7,7,2048]{3,0,2,1:T(2,128)(2,1)S(1)}, bf16[2,7,7,2048]{3,0,2,1:T(2,128)(2,1)}, u32[]{:S(2)}) copy-start(bf16[2,7,7,2048]{3,0,2,1:T(2,128)(2,1)} %param.16) | copy-start | bytes 1204228
  62.1 6.7 %collective-permute-start.4 = (bf16[3,48,512]{2,1,0:T(8,128)(2,1)S(1)}, bf16[3,48,512]{2,1,0:T(8,128)(2,1)S(1)}, u32[]{:S(2)}, u32[]{:S(2)}) collective-permute-start(bf16[3,48,512]{2,1,0:T(8,128)(2,1)S(1)} %get-tuple-element.30), channel_id=1, source_target_pairs={{0,1},{1,2},{2,3},{4,5},{5,6},{6,7},{8,9},{9,10},{10,11},{12,13},{... | collective-permute-start | bytes 442376 | tf_op jit(solution)/shard_map/ppermute | solution.py:36
  65.5 7.9 %collective-permute-start.5 = (bf16[3,48,512]{2,1,0:T(8,128)(2,1)S(1)}, bf16[3,48,512]{2,1,0:T(8,128)(2,1)S(1)}, u32[]{:S(2)}, u32[]{:S(2)}) collective-permute-start(bf16[3,48,512]{2,1,0:T(8,128)(2,1)S(1)} %get-tuple-element.29), channel_id=1, source_target_pairs={{1,0},{2,1},{3,2},{5,4},{6,5},{7,6},{9,8},{10,9},{11,10},{13,12},{... | collective-permute-start | bytes 442376 | tf_op jit(solution)/shard_map/ppermute | solution.py:37
  73.6 6.3 %collective-permute-start.6 = (bf16[30,3,512]{2,1,0:T(4,128)(2,1)S(1)}, bf16[30,3,512]{2,1,0:T(4,128)(2,1)S(1)}, u32[]{:S(2)}, u32[]{:S(2)}) collective-permute-start(bf16[30,3,512]{2,1,0:T(4,128)(2,1)S(1)} %get-tuple-element.23), channel_id=1, source_target_pairs={{0,4},{4,8},{8,12},{12,16},{16,20},{20,24},{24,28},{28,0},{1,5},{5... | collective-permute-start | bytes 276488 | tf_op jit(solution)/shard_map/ppermute | solution.py:36
  74.1 5.7 %collective-permute-start.7 = (bf16[30,3,512]{2,1,0:T(4,128)(2,1)S(1)}, bf16[30,3,512]{2,1,0:T(4,128)(2,1)S(1)}, u32[]{:S(2)}, u32[]{:S(2)}) collective-permute-start(bf16[30,3,512]{2,1,0:T(4,128)(2,1)S(1)} %get-tuple-element.24), channel_id=1, source_target_pairs={{4,0},{8,4},{12,8},{16,12},{20,16},{24,20},{28,24},{0,28},{5,1},{9... | collective-permute-start | bytes 276488 | tf_op jit(solution)/shard_map/ppermute | solution.py:37
  135.1 11.0 %copy-start.2 = (bf16[24,48,512]{2,1,0:T(8,128)(2,1)S(1)}, bf16[24,48,512]{2,1,0:T(8,128)(2,1)}, u32[]{:S(2)}) copy-start(bf16[24,48,512]{2,1,0:T(8,128)(2,1)} %get-tuple-element.13.own_ref) | copy-start | bytes 3538948
  136.3 9.7 %collective-permute-start.8 = (bf16[6,48,512]{2,1,0:T(8,128)(2,1)S(1)}, bf16[6,48,512]{2,1,0:T(8,128)(2,1)S(1)}, u32[]{:S(2)}, u32[]{:S(2)}) collective-permute-start(bf16[6,48,512]{2,1,0:T(8,128)(2,1)S(1)} %get-tuple-element.28), channel_id=1, source_target_pairs={{0,1},{1,2},{2,3},{4,5},{5,6},{6,7},{8,9},{9,10},{10,11},{12,13},{... | collective-permute-start | bytes 884744 | tf_op jit(solution)/shard_map/ppermute | solution.py:36
  138.8 13.7 %collective-permute-start.9 = (bf16[6,48,512]{2,1,0:T(8,128)(2,1)S(1)}, bf16[6,48,512]{2,1,0:T(8,128)(2,1)S(1)}, u32[]{:S(2)}, u32[]{:S(2)}) collective-permute-start(bf16[6,48,512]{2,1,0:T(8,128)(2,1)S(1)} %get-tuple-element.27), channel_id=1, source_target_pairs={{1,0},{2,1},{3,2},{5,4},{6,5},{7,6},{9,8},{10,9},{11,10},{13,12},{... | collective-permute-start | bytes 884744 | tf_op jit(solution)/shard_map/ppermute | solution.py:37
  152.7 10.5 %collective-permute-start.10 = (bf16[36,6,512]{2,1,0:T(8,128)(2,1)S(1)}, bf16[36,6,512]{2,1,0:T(8,128)(2,1)S(1)}, u32[]{:S(2)}, u32[]{:S(2)}) collective-permute-start(bf16[36,6,512]{2,1,0:T(8,128)(2,1)S(1)} %get-tuple-element.17), channel_id=1, source_target_pairs={{0,4},{4,8},{8,12},{12,16},{16,20},{20,24},{24,28},{28,0},{1,5},{5... | collective-permute-start | bytes 663560 | tf_op jit(solution)/shard_map/ppermute | solution.py:36
  152.9 10.2 %collective-permute-start.11 = (bf16[36,6,512]{2,1,0:T(8,128)(2,1)S(1)}, bf16[36,6,512]{2,1,0:T(8,128)(2,1)S(1)}, u32[]{:S(2)}, u32[]{:S(2)}) collective-permute-start(bf16[36,6,512]{2,1,0:T(8,128)(2,1)S(1)} %get-tuple-element.18), channel_id=1, source_target_pairs={{4,0},{8,4},{12,8},{16,12},{20,16},{24,20},{28,24},{0,28},{5,1},{9... | collective-permute-start | bytes 663560 | tf_op jit(solution)/shard_map/ppermute | solution.py:37
  193.8 4.9 %collective-permute-start.12 = (bf16[3,48,512]{2,1,0:T(8,128)(2,1)S(1)}, bf16[3,48,512]{2,1,0:T(8,128)(2,1)S(1)}, u32[]{:S(2)}, u32[]{:S(2)}) collective-permute-start(bf16[3,48,512]{2,1,0:T(8,128)(2,1)S(1)} %get-tuple-element.26), channel_id=1, source_target_pairs={{0,1},{1,2},{2,3},{4,5},{5,6},{6,7},{8,9},{9,10},{10,11},{12,13},{... | collective-permute-start | bytes 442376 | tf_op jit(solution)/shard_map/ppermute | solution.py:36
  195.6 7.2 %collective-permute-start.13 = (bf16[3,48,512]{2,1,0:T(8,128)(2,1)S(1)}, bf16[3,48,512]{2,1,0:T(8,128)(2,1)S(1)}, u32[]{:S(2)}, u32[]{:S(2)}) collective-permute-start(bf16[3,48,512]{2,1,0:T(8,128)(2,1)S(1)} %get-tuple-element.25), channel_id=1, source_target_pairs={{1,0},{2,1},{3,2},{5,4},{6,5},{7,6},{9,8},{10,9},{11,10},{13,12},{... | collective-permute-start | bytes 442376 | tf_op jit(solution)/shard_map/ppermute | solution.py:37
  203.0 6.2 %collective-permute-start.14 = (bf16[30,3,512]{2,1,0:T(4,128)(2,1)S(1)}, bf16[30,3,512]{2,1,0:T(4,128)(2,1)S(1)}, u32[]{:S(2)}, u32[]{:S(2)}) collective-permute-start(bf16[30,3,512]{2,1,0:T(4,128)(2,1)S(1)} %get-tuple-element.21), channel_id=1, source_target_pairs={{0,4},{4,8},{8,12},{12,16},{16,20},{20,24},{24,28},{28,0},{1,5},{5... | collective-permute-start | bytes 276488 | tf_op jit(solution)/shard_map/ppermute | solution.py:36
  203.1 6.1 %collective-permute-start.15 = (bf16[30,3,512]{2,1,0:T(4,128)(2,1)S(1)}, bf16[30,3,512]{2,1,0:T(4,128)(2,1)S(1)}, u32[]{:S(2)}, u32[]{:S(2)}) collective-permute-start(bf16[30,3,512]{2,1,0:T(4,128)(2,1)S(1)} %get-tuple-element.22), channel_id=1, source_target_pairs={{4,0},{8,4},{12,8},{16,12},{20,16},{24,20},{28,24},{0,28},{5,1},{9... | collective-permute-start | bytes 276488 | tf_op jit(solution)/shard_map/ppermute | solution.py:37
